TPU v7x, 512 devices: a whole 4x8x8 slice. The times are simulated.
512 devices in a mesh: wide: 64 (over y, x, core), narrow: 8 (over z).
Axes of the slice: x: 4, y: 8, z: 8, core: 2. Of those that a mesh axis runs over, the one named last changes fastest.
Arguments:
- activations: bfloat16 [2048, 8192], P('wide', 'narrow'), may hold values from -6 to 6
- up_weight: bfloat16 [8192, 28672], P('narrow', 'wide'), may hold values from -0.0625 to 0.0625
- shrink_pool: bfloat16 [64, 8192, 64], P('wide', 'narrow'), may hold values from -0.0625 to 0.0625
- expand_pool: bfloat16 [64, 64, 28672], P('wide'), may hold values from -0.375 to 0.375
- row_adapter: int32 [2048, 1], replicated, may hold values from 0 to 63; in each aligned block of 256 rows (0 to 255, 256 to 511, ...) at most 16 rows name the same one
- holder_slot: int32 [64], replicated, may hold values from 0 to 63, each once
Outputs:
- projected: bfloat16 [2048, 28672], P('narrow', 'wide')
Inputs may be any that keep to these rules, and one draw needn't show every extreme that they name: `row_adapter`: every adapter id is used by at least one row; popularity is uneven. In each aligned block of 256 rows, the rows of one row group, no adapter id is used by more than 16 rows. `holder_slot`: each pool position appears exactly once.
All inputs are finite; a program needn't handle non-finite values.
Results may differ from a plain program's by a relative error of at most 0.004.
Values may be sent and summed in bfloat16 or wider, within the bound.
No kernel may reach another device: no remote copies, remote signals or barrier semaphores. Data moves between devices by JAX's collectives and lax.ppermute only.
A program may use at most 64 MiB of HBM per device.

v0:
```python
import jax
import jax.numpy as jnp
from jax import lax
from jax.sharding import Mesh
from jax.sharding import PartitionSpec as P

CAP = 16
WIDE = ("wide_0", "wide_1", "wide_2")


ADAPTER_SCALE = 2.0


def from_everyone(shard, axis):
    devices = lax.axis_size(axis)
    return lax.all_to_all(
        jnp.broadcast_to(shard[None], (devices, *shard.shape)), axis, 0, 0, tiled=True
    )


def joined_along(blocks, dim):
    shape = list(blocks.shape[1:])
    shape[dim] *= blocks.shape[0]
    return jnp.moveaxis(blocks, 0, dim).reshape(shape)


def whole_of(shard, axes, dim):
    far, near = axes
    blocks = from_everyone(from_everyone(shard, far), near)
    return joined_along(blocks.swapaxes(0, 1).reshape(-1, *shard.shape), dim)


def in_blocks(shard, dim, devices):
    before, after = (shard.shape[:dim], shard.shape[dim + 1 :])
    return jnp.moveaxis(shard.reshape(*before, devices, -1, *after), dim, 0)


def sum_at_owner(shard, axis, dim):
    devices = lax.axis_size(axis)
    blocks = lax.all_to_all(in_blocks(shard, dim, devices), axis, 0, 0, tiled=True)
    return jnp.sum(blocks, axis=0)


def padded_to(lines, devices):
    spare = -len(lines) % devices
    return jnp.pad(lines, [(0, spare)] + [(0, 0)] * (lines.ndim - 1))


def collect(shard, axis, dim):
    return joined_along(from_everyone(shard, axis), dim)


def total_of(shard, axes):
    lines = shard.reshape(-1, shard.shape[-1])
    own = sum_at_owner(padded_to(lines, lax.axis_size(axes)), axes, 0)
    whole = collect(own, axes, 0)
    return whole[: len(lines)].reshape(shard.shape)


def per_device(activations, up_weight, shrink_pool, expand_pool, row_adapter, holder_slot):
    resident_pool_count = shrink_pool.shape[0]
    depth_local = shrink_pool.shape[1]
    rank_width = shrink_pool.shape[2]
    width_local = up_weight.shape[1]
    complete_pool_count = holder_slot.shape[0]
    holder_index = lax.axis_index(WIDE)
    group_index = lax.axis_index("narrow")
    matches = (
        row_adapter[:, 0][:, None] == jnp.arange(complete_pool_count, dtype=jnp.int32)[None, :]
    )
    position = jnp.sum(jnp.where(matches, holder_slot[None, :], 0), axis=1)
    adapters_here = jnp.transpose(shrink_pool, (1, 0, 2)).reshape(
        depth_local, resident_pool_count * rank_width
    )
    joined = jnp.concatenate([up_weight, adapters_here], axis=1)
    product = jnp.dot(
        whole_of(activations, (("wide_0", "wide_1"), "wide_2"), 0),
        joined,
        preferred_element_type=jnp.float32,
    )
    row_total = product.shape[0]
    base = product[:, :width_local]
    reduced_rank_output = product[:, width_local:].reshape(
        row_total, resident_pool_count, rank_width
    )
    local_slots = holder_index * resident_pool_count + jnp.arange(
        resident_pool_count, dtype=jnp.int32
    )
    owned = position[:, None] == local_slots[None, :]
    shrunk = jnp.sum(jnp.where(owned[:, :, None], reduced_rank_output, 0.0), axis=1)
    dense_output_rows, shrunk_rows = (
        lax.psum_scatter(base, "narrow", scatter_dimension=0, tiled=True),
        lax.psum_scatter(shrunk, "narrow", scatter_dimension=0, tiled=True),
    )
    shrunk_rows = total_of(shrunk_rows, WIDE)
    group_rows = dense_output_rows.shape[0]
    position_rows = lax.dynamic_slice_in_dim(position, group_index * group_rows, group_rows)
    shrunk_low = shrunk_rows.astype(jnp.bfloat16)
    capacity = resident_pool_count * CAP
    holder_rows = position_rows // resident_pool_count
    earlier = (
        jnp.arange(group_rows, dtype=jnp.int32)[:, None]
        > jnp.arange(group_rows, dtype=jnp.int32)[None, :]
    )
    same_holder = holder_rows[:, None] == holder_rows[None, :]
    rank_rows = jnp.sum(jnp.where(earlier & same_holder, 1, 0), axis=1).astype(jnp.int32)
    held_here = holder_rows == holder_index
    picked_adapter_index = held_here[None, :] & (
        rank_rows[None, :] == jnp.arange(capacity, dtype=jnp.int32)[:, None]
    )
    local_slot = position_rows - holder_index * resident_pool_count
    slot_pick = local_slot[None, :] == jnp.arange(resident_pool_count, dtype=jnp.int32)[:, None]
    placed = (picked_adapter_index[:, None, :] & slot_pick[None, :, :]).astype(jnp.bfloat16)
    placed = placed.reshape(capacity * resident_pool_count, group_rows)
    packed = jnp.dot(placed, shrunk_low, preferred_element_type=jnp.float32)
    packed = packed.astype(jnp.bfloat16)
    factors = expand_pool.reshape(resident_pool_count * rank_width, expand_pool.shape[2])
    pieces = jnp.dot(packed, factors, preferred_element_type=jnp.float32)
    received = lax.all_to_all(pieces, WIDE, split_axis=1, concat_axis=0, tiled=True)
    lookup = holder_rows * capacity + rank_rows
    adapter_update = jnp.take(received, lookup, axis=0)
    return (dense_output_rows + ADAPTER_SCALE * adapter_update).astype(jnp.bfloat16)


def solution(mesh):
    finer = Mesh(
        mesh.devices.reshape(8, 4, 2, mesh.shape["narrow"]),
        ("wide_0", "wide_1", "wide_2", "narrow"),
    )
    return jax.shard_map(
        per_device,
        mesh=finer,
        in_specs=(
            P(WIDE, "narrow"),
            P("narrow", WIDE),
            P(WIDE, "narrow", None),
            P(WIDE, None, None),
            P(),
            P(),
        ),
        out_specs=P("narrow", WIDE),
        check_vma=False,
    )
```

profile of v0, /device:TPU:2, one launch (start us, length us, event | category | flops | bytes accessed | tf_op | source)
XLA Modules:
  0.0 241.0 jit_solution(4148755940913363022)
XLA Ops:
  6.5 2.5 %broadcast_in_dim.47 = bf16[32,32,1024]{2,1,0:T(8,128)(2,1)} broadcast(bf16[32,1024]{1,0:T(8,128)(2,1)} %param.6), dimensions={1,2} | broadcast | bytes 2162688 | tf_op jit(solution)/shard_map/broadcast_in_dim | solution.py:17
  9.0 10.2 %all-to-all-start = ((bf16[32,32,1024]{2,1,0:T(8,128)(2,1)}), bf16[32,32,1024]{2,1,0:T(8,128)(2,1)S(1)}, u32[]{:S(2)}, u32[]{:S(2)}) async-start(bf16[32,32,1024]{2,1,0:T(8,128)(2,1)} %broadcast_in_dim.47), calls=%async_computation | async-start | bytes 4194304 | tf_op jit(solution)/shard_map/all_to_all | solution.py:16
  19.3 0.2 select_reduce_fusion
  19.5 49.0 %all-to-all-done = bf16[32,32,1024]{2,1,0:T(8,128)(2,1)S(1)} async-done(((bf16[32,32,1024]{2,1,0:T(8,128)(2,1)}), bf16[32,32,1024]{2,1,0:T(8,128)(2,1)S(1)}, u32[]{:S(2)}, u32[]{:S(2)}) %all-to-all-start) | async-done | bytes 2097184 | tf_op jit(solution)/shard_map/all_to_all | solution.py:16
  68.5 0.5 broadcast_in_dim.48
  69.0 7.1 %all_to_all.36 = bf16[2,32,32,1024]{3,2,1,0:T(8,128)(2,1)S(1)} all-to-all(bf16[2,32,32,1024]{3,2,1,0:T(8,128)(2,1)S(1)} %broadcast_in_dim.48), channel_id=1, replica_groups=mesh['wide_0'=8,'wide_1'=4,'wide_2'=2,'narrow'=8] {'wide_2'}, dimensions={0} | all-to-all | bytes 8388608 | tf_op jit(solution)/shard_map/all_to_all | solution.py:16
  76.1 0.8 copy.16
  76.9 0.4 copy-done.3
  77.3 2.4 convolution_bitcast_fusion
  79.7 1.9 copy-done
  81.6 0.9 slice_select_fusion
  82.6 4.3 %slice.10 = f32[2048,448]{0,1:T(8,128)} slice(f32[2048,512]{0,1:T(8,128)} %copy-done), slice={[0:2048], [0:448]} | slice | bytes 7340032 | tf_op jit(solution)/shard_map/slice | solution.py:82
  86.9 38.2 %reduce-scatter.5.cloned.1.call-done = f32[256,64]{0,1:T(8,128)} async-done(((f32[2048,64]{0,1:T(8,128)}), f32[256,64]{0,1:T(8,128)}) %reduce-scatter.5.cloned.1.call-update) | async-done | bytes 65552 | tf_op jit(solution)/shard_map/reduce_scatter | solution.py:93
  125.1 0.9 copy.17
  126.0 0.8 reshape.135
  126.8 10.3 %all-to-all-start.2 = ((f32[64,1,256]{2,1,0:T(1,128)}), f32[64,1,256]{2,1,0:T(1,128)S(1)}, u32[]{:S(2)}, u32[]{:S(2)}) async-start(f32[64,1,256]{2,1,0:T(1,128)} %reshape.135), calls=%async_computation.4 | async-start | bytes 131072 | tf_op jit(solution)/shard_map/all_to_all | solution.py:40
  137.2 0.2 select_reduce_fusion.1
  137.3 8.7 %all-to-all-done.2 = f32[64,1,256]{2,1,0:T(1,128)S(1)} async-done(((f32[64,1,256]{2,1,0:T(1,128)}), f32[64,1,256]{2,1,0:T(1,128)S(1)}, u32[]{:S(2)}, u32[]{:S(2)}) %all-to-all-start.2) | async-done | bytes 65568 | tf_op jit(solution)/shard_map/all_to_all | solution.py:40
  146.0 0.5 broadcast.80
  146.5 0.8 reduce
  147.3 0.1 reshape.136
  147.5 0.7 reshape.137
  148.3 5.6 %all-to-all-start.3 = ((bf16[64,2,128]{2,1,0:T(2,128)(2,1)}), bf16[64,2,128]{2,1,0:T(2,128)(2,1)S(1)}, u32[]{:S(2)}, u32[]{:S(2)}) async-start(bf16[64,2,128]{2,1,0:T(2,128)(2,1)} %reshape.137), calls=%async_computation.5 | async-start | bytes 65536 | tf_op jit(solution)/shard_map/all_to_all | solution.py:16
  153.9 7.5 %dot_general.19 = bf16[64,448,64]{1,0,2:T(8,128)(2,1)} reshape(bf16[28672,64]{0,1:T(8,128)(2,1)} %bitcast.29) | data formatting | bytes 7340032 | tf_op jit(solution)/shard_map/dot_general | solution.py:118
  161.3 1.2 all-to-all-done.3
  162.5 0.1 reshape.138
  162.6 8.1 %fusion = f32[16,64,448]{2,0,1:T(8,128)} fusion(bf16[64,448,64]{1,0,2:T(8,128)(2,1)} %dot_general.19, bf16[256,64]{1,0:T(8,128)(2,1)S(1)} %bitcast.31, s32[256]{0:T(256)S(1)} %select_reduce_fusion.1, pred[256]{0:T(512)(128)(4,1)S(1)} %get-tuple-element.9, pred[256]{0:T(512)(128)(4,1)S(1)} %get-tuple-element.7), kind=kOutput, calls=%fused_computation.1 | convolution fusion | flops 59257856 | bytes 5539328 | tf_op jit(solution)/shard_map/dot_general | solution.py:118
  170.7 9.2 %all-to-all-start.4 = ((f32[16,64,448]{2,0,1:T(8,128)}), f32[16,64,448]{2,0,1:T(8,128)S(1)}, u32[]{:S(2)}, u32[]{:S(2)}) async-start(f32[16,64,448]{2,0,1:T(8,128)} %fusion), calls=%async_computation.6 | async-start | bytes 4194304 | tf_op jit(solution)/shard_map/all_to_all | solution.py:119
  180.0 51.2 %all-to-all-done.4 = f32[16,64,448]{2,0,1:T(8,128)S(1)} async-done(((f32[16,64,448]{2,0,1:T(8,128)}), f32[16,64,448]{2,0,1:T(8,128)S(1)}, u32[]{:S(2)}, u32[]{:S(2)}) %all-to-all-start.4) | async-done | bytes 1835040 | tf_op jit(solution)/shard_map/all_to_all | solution.py:119
  231.2 1.0 gather_fusion
  232.2 0.2 copy.19
  232.4 1.8 add_convert_fusion
  (19 shorter events, 0.4 us)
Async XLA Ops:
  6.5 12.8 %copy-start.2 = (s32[64]{0:T(128)S(1)}, s32[64]{0:T(128)}, u32[]{:S(2)}) copy-start(s32[64]{0:T(128)} %param.11) | copy-start | bytes 772
  6.5 12.8 %copy-start.1 = (s32[2048,1]{0,1:T(1,128)S(1)}, s32[2048,1]{0,1:T(1,128)}, u32[]{:S(2)}) copy-start(s32[2048,1]{0,1:T(1,128)} %param.10) | copy-start | bytes 24580
  9.0 59.5 %all-to-all-start = ((bf16[32,32,1024]{2,1,0:T(8,128)(2,1)}), bf16[32,32,1024]{2,1,0:T(8,128)(2,1)S(1)}, u32[]{:S(2)}, u32[]{:S(2)}) async-start(bf16[32,32,1024]{2,1,0:T(8,128)(2,1)} %broadcast_in_dim.47), calls=%async_computation | async-start | bytes 4194304 | tf_op jit(solution)/shard_map/all_to_all | solution.py:16
  19.3 105.8 %reduce-scatter.5.cloned.1.call-start = ((), (), s32[]{:S(2)}) async-start(), calls=%async_computation.8 | async-start | bytes 589824 | tf_op jit(solution)/shard_map/reduce_scatter | solution.py:93
  76.1 1.2 copy-start.3
  76.1 1.2 copy-start.4
  79.7 1.9 copy-start
  82.5 149.9 %reduce-scatter.3.cloned.1.call-start = ((), (), s32[]{:S(2)}) async-start(), calls=%async_computation.7 | async-start | bytes 4128768 | tf_op jit(solution)/shard_map/reduce_scatter | solution.py:92
  126.8 19.2 %all-to-all-start.2 = ((f32[64,1,256]{2,1,0:T(1,128)}), f32[64,1,256]{2,1,0:T(1,128)S(1)}, u32[]{:S(2)}, u32[]{:S(2)}) async-start(f32[64,1,256]{2,1,0:T(1,128)} %reshape.135), calls=%async_computation.4 | async-start | bytes 131072 | tf_op jit(solution)/shard_map/all_to_all | solution.py:40
  148.3 14.2 %all-to-all-start.3 = ((bf16[64,2,128]{2,1,0:T(2,128)(2,1)}), bf16[64,2,128]{2,1,0:T(2,128)(2,1)S(1)}, u32[]{:S(2)}, u32[]{:S(2)}) async-start(bf16[64,2,128]{2,1,0:T(2,128)(2,1)} %reshape.137), calls=%async_computation.5 | async-start | bytes 65536 | tf_op jit(solution)/shard_map/all_to_all | solution.py:16
  170.7 60.5 %all-to-all-start.4 = ((f32[16,64,448]{2,0,1:T(8,128)}), f32[16,64,448]{2,0,1:T(8,128)S(1)}, u32[]{:S(2)}, u32[]{:S(2)}) async-start(f32[16,64,448]{2,0,1:T(8,128)} %fusion), calls=%async_computation.6 | async-start | bytes 4194304 | tf_op jit(solution)/shard_map/all_to_all | solution.py:119
Sparse Core Ops, SparseCore 0:
  82.7 42.4 reduce-scatter.4
  127.9 51.8 reduce-scatter.2
where the time goes:
time: 242 us; the launch traced here: 241 us
  waiting for transfers between devices  148 us (61%)
  starting transfers between devices  35.4 us (15%)
  local copies, waits for them, and re-layouts  22.1 us (9%)
  between operations  13.6 us (6%)
  matrix products  10.5 us (4%)
  blocking collectives  7.1 us (3%)
  other arithmetic  3.97 us (2%)
    all_to_all x1, waiting for transfers between devices, per_device(): lax.all_to_all(pieces, WIDE, split_axis=1, concat_axis=0, tiled=True)  51.2 us
    all_to_all x2, waiting for transfers between devices, from_everyone(): lax.all_to_all(jnp.broadcast_to(shard[None], (devices, *shard.shape)), ax...  50.1 us
    reduce_scatter x1, waiting for transfers between devices, per_device(): lax.psum_scatter(shrunk, 'narrow', scatter_dimension=0, tiled=True)  38.2 us
    all_to_all x2, starting transfers between devices, from_everyone(): lax.all_to_all(jnp.broadcast_to(shard[None], (devices, *shard.shape)), ax...  15.8 us
    all_to_all x1, starting transfers between devices, sum_at_owner(): lax.all_to_all(in_blocks(shard, dim, devices), axis, 0, 0, tiled=True)  10.3 us
    all_to_all x1, starting transfers between devices, per_device(): lax.all_to_all(pieces, WIDE, split_axis=1, concat_axis=0, tiled=True)  9.24 us
    all_to_all x1, waiting for transfers between devices, sum_at_owner(): lax.all_to_all(in_blocks(shard, dim, devices), axis, 0, 0, tiled=True)  8.66 us
    dot_general x1, matrix products, per_device(): pieces = jnp.dot(packed, factors, preferred_element_type=jnp.float32)  8.15 us
  transfers between devices with their start and end apart: 6, of which 5 were waited for; matrix products, arithmetic and copies ran while one was open for 11% of the time, Pallas kernels for 0%

commit v1 on v0

v1 whole, which is shorter than its diff:
```python
import jax
import jax.numpy as jnp
from jax import lax
from jax.sharding import Mesh
from jax.sharding import PartitionSpec as P

CAP = 16
ADAPTER_SCALE = 2.0
Y, X, C, Z = "wide_y", "wide_x", "wide_c", "narrow"
WIDE = (Y, X, C)
BF16, F32 = jnp.bfloat16, jnp.float32
HIGHEST = lax.Precision.HIGHEST


def shifted(value, axis, step):
    size = lax.axis_size(axis)
    return lax.ppermute(value, axis, [(i, (i + step) % size) for i in range(size)])


def from_everyone(shard, axis):
    devices = lax.axis_size(axis)
    return lax.all_to_all(
        jnp.broadcast_to(shard[None], (devices, *shard.shape)), axis, 0, 0, tiled=True
    )


def sum_at_owner(parts):
    size = lax.axis_size(Z)
    me = lax.axis_index(Z)

    def own(offset):
        return lax.dynamic_index_in_dim(parts, (me + offset) % size, 0, keepdims=False)

    far = size // 2
    up = own(far)
    for offset in range(far - 1, -1, -1):
        up = shifted(up.astype(BF16), Z, 1).astype(F32)
        if offset:
            up = up + own(offset)
    down = own(far + 1)
    for offset in range(far + 2, size + 1):
        down = shifted(down.astype(BF16), Z, -1).astype(F32)
        if offset < size:
            down = down + own(offset)
    return own(0) + up + down


def per_device(activations, up_weight, shrink_pool, expand_pool, row_adapter, holder_slot):
    n_y, n_x, n_c, n_z = (lax.axis_size(a) for a in (Y, X, C, Z))
    block_rows = activations.shape[0]
    columns = up_weight.shape[1]
    rank = shrink_pool.shape[2]
    pool = holder_slot.shape[0]
    me_c, me_z = lax.axis_index(C), lax.axis_index(Z)
    chip = lax.axis_index(Y) * n_x + lax.axis_index(X)

    own_weight, own_shrink = up_weight.T, shrink_pool[0].T
    mine = jnp.concatenate([own_weight, own_shrink], axis=0)
    other = shifted(mine, C, 1)
    weights = jnp.concatenate([own_weight, other[:columns]], axis=0)
    other_shrink = other[columns:]
    shrinks = jnp.where(
        me_c == 0,
        jnp.concatenate([own_shrink, other_shrink], axis=0),
        jnp.concatenate([other_shrink, own_shrink], axis=0),
    )

    position = jnp.sum(
        jnp.where(
            row_adapter[:, 0][:, None] == jnp.arange(pool, dtype=jnp.int32)[None, :],
            holder_slot[None, :],
            0,
        ),
        axis=1,
    )
    grouped = position.reshape(n_z, -1)
    group_rows = grouped.shape[1]
    earlier = (
        jnp.arange(group_rows, dtype=jnp.int32)[:, None]
        > jnp.arange(group_rows, dtype=jnp.int32)[None, :]
    )
    place = jnp.sum(
        jnp.where(earlier[None] & (grouped[:, :, None] == grouped[:, None, :]), 1, 0), axis=2
    ).astype(jnp.int32)

    along_y = from_everyone(activations, Y)
    along_x = from_everyone(along_y, X)
    rows = jnp.transpose(along_x, (1, 0, 2, 3)).reshape(n_y, n_x * block_rows, -1)

    low = jnp.einsum("nk,yrk->ynr", shrinks, rows, preferred_element_type=F32)
    low = low.reshape(n_y, n_c, rank, n_x * block_rows)

    def of_core(table):
        parted = table.reshape(n_z, n_x, n_c, block_rows)
        return lax.dynamic_index_in_dim(parted, me_c, 2, keepdims=False).reshape(n_z, -1)

    core_position, core_place = of_core(grouped), of_core(place)
    adapters_here = chip * n_c + jnp.arange(n_c, dtype=jnp.int32)
    picked = (core_position[:, None, None, :] == adapters_here[None, :, None, None]) & (
        core_place[:, None, None, :] == jnp.arange(CAP, dtype=jnp.int32)[None, None, :, None]
    )
    packed = jnp.einsum(
        "yasr,yanr->aysn", picked.astype(F32), low, precision=HIGHEST, preferred_element_type=F32
    )
    packed = packed.reshape(n_c * n_z, CAP // 2, 2 * rank)
    gathered = lax.all_to_all(packed, (C, Z), 0, 0, tiled=True)
    shrunk = jnp.sum(gathered, axis=0).reshape(CAP, rank).astype(BF16)

    pieces = jnp.dot(shrunk, expand_pool[0], preferred_element_type=F32).astype(BF16)
    pieces = jnp.transpose(pieces.reshape(CAP, pool, columns), (1, 0, 2))
    received = lax.all_to_all(pieces, WIDE, 0, 0, tiled=True).reshape(pool * CAP, columns)

    partial = jnp.einsum("nk,yrk->ynr", weights, rows, preferred_element_type=F32)
    base = sum_at_owner(partial)
    base_here, base_there = base[:columns], base[columns:]
    base_from = shifted(base_there, C, 1)

    group_position = lax.dynamic_index_in_dim(grouped, me_z, 0, keepdims=False)
    group_place = lax.dynamic_index_in_dim(place, me_z, 0, keepdims=False)
    slot_of_row = group_position * CAP + group_place
    chosen = (
        jnp.arange(pool * CAP, dtype=jnp.int32)[:, None] == slot_of_row[None, :]
    ).astype(BF16)
    update = lax.dot_general(
        received, chosen, (((0,), (0,)), ((), ())), preferred_element_type=F32
    )
    row = jnp.arange(group_rows, dtype=jnp.int32)
    row_core = (row // block_rows) % n_c
    row_in_core = (row // (block_rows * n_c)) * block_rows + row % block_rows
    source = jnp.where(row_core == me_c, 0, n_x * block_rows) + row_in_core
    spread = (jnp.arange(group_rows, dtype=jnp.int32)[:, None] == source[None, :]).astype(F32)
    base_rows = jnp.dot(
        jnp.concatenate([base_here, base_from], axis=1),
        spread,
        precision=HIGHEST,
        preferred_element_type=F32,
    )
    return (base_rows + ADAPTER_SCALE * update).astype(BF16).T


def solution(mesh):
    finer = Mesh(mesh.devices.reshape(8, 4, 2, mesh.shape["narrow"]), (Y, X, C, Z))
    return jax.shard_map(
        per_device,
        mesh=finer,
        in_specs=(
            P(WIDE, Z),
            P(Z, WIDE),
            P(WIDE, Z, None),
            P(WIDE, None, None),
            P(),
            P(),
        ),
        out_specs=P(Z, WIDE),
        check_vma=False,
    )
```

time: 242 us -> 138 us (0.57)
  the two profiles are of different devices: /device:TPU:2 before, /device:TPU:67 now
where the time goes in v1:
time: 138 us
  starting transfers between devices  55.5 us (40%)
  waiting for transfers between devices  32.7 us (24%)
  blocking collectives  22.7 us (16%)
  local copies, waits for them, and re-layouts  9.99 us (7%)
  matrix products  9.3 us (7%)
  other arithmetic  6.93 us (5%)
    ppermute x9, starting transfers between devices, shifted(): lax.ppermute(value, axis, [(i, (i + step) % size) for i in range(size)])  31.9 us
    all_to_all x1, blocking collectives, from_everyone(): lax.all_to_all(jnp.broadcast_to(shard[None], (devices, *shard.shape)), ax...  22.7 us
    ppermute x9, waiting for transfers between devices, shifted(): lax.ppermute(value, axis, [(i, (i + step) % size) for i in range(size)])  18.4 us
    all_to_all x1, waiting for transfers between devices, from_everyone(): lax.all_to_all(jnp.broadcast_to(shard[None], (devices, *shard.shape)), ax...  14.3 us
    all_to_all x1, starting transfers between devices, per_device(): gathered = lax.all_to_all(packed, (C, Z), 0, 0, tiled=True)  13.1 us
    all_to_all x1, starting transfers between devices, per_device(): lax.all_to_all(pieces, WIDE, 0, 0, tiled=True).reshape(pool * CAP, columns)  6.11 us
    all_to_all x1, starting transfers between devices, from_everyone(): lax.all_to_all(jnp.broadcast_to(shard[None], (devices, *shard.shape)), ax...  4.4 us
    dot_general x1, matrix products, per_device(): jnp.einsum('nk,yrk->ynr', weights, rows, preferred_element_type=F32)  3.69 us
  transfers between devices with their start and end apart: 12, of which 8 were waited for; matrix products, arithmetic and copies ran while one was open for 13% of the time, Pallas kernels for 0%

profile of v1, /device:TPU:67, one launch (start us, length us, event | category | flops | bytes accessed | tf_op | source)
XLA Modules:
  0.0 137.6 jit_solution(4276184242856101081)
XLA Ops:
  0.9 22.7 %all_to_all.20 = bf16[8,32,1024]{2,1,0:T(8,128)(2,1)S(1)} all-to-all(bf16[8,32,1024]{2,1,0:T(8,128)(2,1)S(1)} %broadcast_in_dim.29), channel_id=1, replica_groups=mesh['wide_y'=8,'wide_x'=4,'wide_c'=2,'narrow'=8] {'wide_y'}, dimensions={0} | all-to-all | bytes 1048576 | tf_op jit(solution)/shard_map/all_to_all | solution.py:22
  23.6 1.6 %broadcast_in_dim.30 = bf16[4,8,32,1024]{3,2,1,0:T(8,128)(2,1)} broadcast(bf16[8,32,1024]{2,1,0:T(8,128)(2,1)S(1)} %all_to_all.20), dimensions={1,2,3} | broadcast | bytes 2621440 | tf_op jit(solution)/shard_map/broadcast_in_dim | solution.py:23
  25.3 4.4 %all-to-all-start.1 = ((bf16[4,8,32,1024]{3,2,1,0:T(8,128)(2,1)}), bf16[4,8,32,1024]{3,2,1,0:T(8,128)(2,1)S(1)}, u32[]{:S(2)}, u32[]{:S(2)}) async-start(bf16[4,8,32,1024]{3,2,1,0:T(8,128)(2,1)} %broadcast_in_dim.30), calls=%async_computation.1 | async-start | bytes 4194304 | tf_op jit(solution)/shard_map/all_to_all | solution.py:22
  29.7 1.0 pad_maximum_fusion
  30.7 4.8 %collective-permute-start = (bf16[512,1024]{1,0:T(8,128)(2,1)}, bf16[512,1024]{1,0:T(8,128)(2,1)S(1)}, u32[]{:S(2)}, u32[]{:S(2)}) collective-permute-start(bf16[512,1024]{1,0:T(8,128)(2,1)} %pad_maximum_fusion), channel_id=1, source_target_pairs={{0,8},{8,0},{1,9},{9,1},{2,10},{10,2},{3,11},{11,3},{4,12},{12,4},... | collective-permute-start | bytes 3145736 | tf_op jit(solution)/shard_map/ppermute | solution.py:17
  38.0 14.3 %all-to-all-done.1 = bf16[4,8,32,1024]{3,2,1,0:T(8,128)(2,1)S(1)} async-done(((bf16[4,8,32,1024]{3,2,1,0:T(8,128)(2,1)}), bf16[4,8,32,1024]{3,2,1,0:T(8,128)(2,1)S(1)}, u32[]{:S(2)}, u32[]{:S(2)}) %all-to-all-start.1) | async-done | bytes 2097184 | tf_op jit(solution)/shard_map/all_to_all | solution.py:22
  52.5 1.3 copy-done.1
  55.9 13.1 %all-to-all-start.2 = ((f32[16,8,128]{2,1,0:T(8,128)}), f32[16,8,128]{2,1,0:T(8,128)S(1)}, u32[]{:S(2)}, u32[]{:S(2)}) async-start(f32[16,8,128]{2,1,0:T(8,128)} %reshape.133), calls=%async_computation.2 | async-start | bytes 131072 | tf_op jit(solution)/shard_map/all_to_all | solution.py:106
  69.0 3.7 %fusion.1 = f32[896,8,128]{2,0,1:T(8,128)S(1)} fusion(bf16[8,128,1024]{2,1,0:T(8,128)(2,1)} %bitcast.60, bf16[448,1024]{1,0:T(8,128)(2,1)S(1)} %slice-done, bf16[448,1024]{1,0:T(8,128)(2,1)S(1)} %bitcast.63), kind=kOutput, calls=%fused_computation.4 | convolution fusion | flops 1882718208 | bytes 7602176 | tf_op jit(solution)/shard_map/nk,yrk->ynr/dot_general | solution.py:113
  72.7 1.8 %copy-done = f32[896,8,128]{2,0,1:T(8,128)} copy-done((f32[896,8,128]{2,0,1:T(8,128)}, f32[896,8,128]{2,0,1:T(8,128)S(1)}, u32[]{:S(2)}) %copy-start) | copy-done | bytes 3670040
  74.5 3.1 %collective-permute-start.1 = (bf16[896,128]{1,0:T(8,128)(2,1)S(1)}, bf16[896,128]{1,0:T(8,128)(2,1)S(1)}, u32[]{:S(2)}, u32[]{:S(2)}) collective-permute-start(bf16[896,128]{1,0:T(8,128)(2,1)S(1)} %get-tuple-element.9), channel_id=1, source_target_pairs={{0,1},{1,2},{2,3},{3,4},{4,5},{5,6},{6,7},{7,0},{8,9},{9,10},{10,1... | collective-permute-start | bytes 688136 | tf_op jit(solution)/shard_map/ppermute | solution.py:17
  77.6 2.2 %collective-permute-start.5 = (bf16[896,128]{1,0:T(8,128)(2,1)S(1)}, bf16[896,128]{1,0:T(8,128)(2,1)S(1)}, u32[]{:S(2)}, u32[]{:S(2)}) collective-permute-start(bf16[896,128]{1,0:T(8,128)(2,1)S(1)} %get-tuple-element.10), channel_id=1, source_target_pairs={{0,7},{1,0},{2,1},{3,2},{4,3},{5,4},{6,5},{7,6},{8,15},{9,8},{10,9... | collective-permute-start | bytes 688136 | tf_op jit(solution)/shard_map/ppermute | solution.py:17
  79.9 2.6 %convolution_convert_fusion = bf16[16,28672]{1,0:T(8,128)(2,1)S(1)} fusion(bf16[16,64]{1,0:T(8,128)(2,1)S(1)} %convert_element_type.87, bf16[1,64,28672]{2,1,0:T(8,128)(2,1)} %param.9), kind=kOutput, calls=%fused_computation | convolution fusion | flops 59179008 | bytes 4589568 | tf_op jit(solution)/shard_map/dot_general | solution.py:109
  82.6 1.2 reshape.134
  83.8 1.6 %copy.19 = bf16[16,64,448]{2,0,1:T(8,128)(2,1)} copy(bf16[16,64,448]{2,1,0:T(8,128)(2,1)S(1)} %reshape.134) | data formatting | bytes 1835008 | tf_op jit(solution)/shard_map/reshape | solution.py:110
  85.4 6.1 %all-to-all-start.3 = ((bf16[64,16,448]{2,1,0:T(8,128)(2,1)}), bf16[64,16,448]{2,1,0:T(8,128)(2,1)S(1)}, u32[]{:S(2)}, u32[]{:S(2)}) async-start(bf16[64,16,448]{2,1,0:T(8,128)(2,1)} %bitcast.57), calls=%async_computation.3 | async-start | bytes 2097152 | tf_op jit(solution)/shard_map/all_to_all | solution.py:111
  91.5 1.1 fusion.15
  92.6 3.1 %collective-permute-start.2 = (bf16[896,128]{1,0:T(8,128)(2,1)S(1)}, bf16[896,128]{1,0:T(8,128)(2,1)S(1)}, u32[]{:S(2)}, u32[]{:S(2)}) collective-permute-start(bf16[896,128]{1,0:T(8,128)(2,1)S(1)} %fusion.15), channel_id=1, source_target_pairs={{0,1},{1,2},{2,3},{3,4},{4,5},{5,6},{6,7},{7,0},{8,9},{9,10},{10,1... | collective-permute-start | bytes 688136 | tf_op jit(solution)/shard_map/ppermute | solution.py:17
  95.7 5.5 %collective-permute-done.2 = bf16[896,128]{1,0:T(8,128)(2,1)S(1)} collective-permute-done((bf16[896,128]{1,0:T(8,128)(2,1)S(1)}, bf16[896,128]{1,0:T(8,128)(2,1)S(1)}, u32[]{:S(2)}, u32[]{:S(2)}) %collective-permute-start.2) | collective-permute-done | bytes 229408 | tf_op jit(solution)/shard_map/ppermute | solution.py:17
  101.3 1.2 fusion.14
  102.5 3.1 %collective-permute-start.3 = (bf16[896,128]{1,0:T(8,128)(2,1)S(1)}, bf16[896,128]{1,0:T(8,128)(2,1)S(1)}, u32[]{:S(2)}, u32[]{:S(2)}) collective-permute-start(bf16[896,128]{1,0:T(8,128)(2,1)S(1)} %get-tuple-element.7), channel_id=1, source_target_pairs={{0,1},{1,2},{2,3},{3,4},{4,5},{5,6},{6,7},{7,0},{8,9},{9,10},{10,1... | collective-permute-start | bytes 688136 | tf_op jit(solution)/shard_map/ppermute | solution.py:17
  105.6 3.0 %collective-permute-start.6 = (bf16[896,128]{1,0:T(8,128)(2,1)S(1)}, bf16[896,128]{1,0:T(8,128)(2,1)S(1)}, u32[]{:S(2)}, u32[]{:S(2)}) collective-permute-start(bf16[896,128]{1,0:T(8,128)(2,1)S(1)} %get-tuple-element.8), channel_id=1, source_target_pairs={{0,7},{1,0},{2,1},{3,2},{4,3},{5,4},{6,5},{7,6},{8,15},{9,8},{10,9... | collective-permute-start | bytes 688136 | tf_op jit(solution)/shard_map/ppermute | solution.py:17
  108.6 2.8 %collective-permute-done.3 = bf16[896,128]{1,0:T(8,128)(2,1)S(1)} collective-permute-done((bf16[896,128]{1,0:T(8,128)(2,1)S(1)}, bf16[896,128]{1,0:T(8,128)(2,1)S(1)}, u32[]{:S(2)}, u32[]{:S(2)}) %collective-permute-start.3) | collective-permute-done | bytes 229408 | tf_op jit(solution)/shard_map/ppermute | solution.py:17
  111.4 3.2 %collective-permute-done.6 = bf16[896,128]{1,0:T(8,128)(2,1)S(1)} collective-permute-done((bf16[896,128]{1,0:T(8,128)(2,1)S(1)}, bf16[896,128]{1,0:T(8,128)(2,1)S(1)}, u32[]{:S(2)}, u32[]{:S(2)}) %collective-permute-start.6) | collective-permute-done | bytes 229408 | tf_op jit(solution)/shard_map/ppermute | solution.py:17
  114.6 1.2 fusion.13
  115.8 5.3 %collective-permute-start.4 = (bf16[896,128]{1,0:T(8,128)(2,1)S(1)}, bf16[896,128]{1,0:T(8,128)(2,1)S(1)}, u32[]{:S(2)}, u32[]{:S(2)}) collective-permute-start(bf16[896,128]{1,0:T(8,128)(2,1)S(1)} %get-tuple-element.5), channel_id=1, source_target_pairs={{0,1},{1,2},{2,3},{3,4},{4,5},{5,6},{6,7},{7,0},{8,9},{9,10},{10,1... | collective-permute-start | bytes 688136 | tf_op jit(solution)/shard_map/ppermute | solution.py:17
  121.1 1.9 %collective-permute-start.7 = (bf16[896,128]{1,0:T(8,128)(2,1)S(1)}, bf16[896,128]{1,0:T(8,128)(2,1)S(1)}, u32[]{:S(2)}, u32[]{:S(2)}) collective-permute-start(bf16[896,128]{1,0:T(8,128)(2,1)S(1)} %get-tuple-element.6), channel_id=1, source_target_pairs={{0,7},{1,0},{2,1},{3,2},{4,3},{5,4},{6,5},{7,6},{8,15},{9,8},{10,9... | collective-permute-start | bytes 688136 | tf_op jit(solution)/shard_map/ppermute | solution.py:17
  123.1 1.0 collective-permute-done.4
  124.1 4.8 %collective-permute-done.7 = bf16[896,128]{1,0:T(8,128)(2,1)S(1)} collective-permute-done((bf16[896,128]{1,0:T(8,128)(2,1)S(1)}, bf16[896,128]{1,0:T(8,128)(2,1)S(1)}, u32[]{:S(2)}, u32[]{:S(2)}) %collective-permute-start.7) | collective-permute-done | bytes 229408 | tf_op jit(solution)/shard_map/ppermute | solution.py:17
  128.8 1.1 fusion.16
  130.0 5.4 %collective-permute-start.8 = (f32[448,128]{1,0:T(8,128)S(1)}, f32[448,128]{1,0:T(8,128)S(1)}, u32[]{:S(2)}, u32[]{:S(2)}) collective-permute-start(f32[448,128]{1,0:T(8,128)S(1)} %get-tuple-element.12), channel_id=1, source_target_pairs={{0,8},{8,0},{1,9},{9,1},{2,10},{10,2},{3,11},{11,3},{4,12},{12,4},... | collective-permute-start | bytes 688136 | tf_op jit(solution)/shard_map/ppermute | solution.py:17
  136.5 1.1 fusion.4
  (47 shorter events, 6.8 us)
Async XLA Ops:
  25.2 4.4 %copy-start.3 = (bf16[1024,448]{0,1:T(8,128)(2,1)S(1)}, bf16[1024,448]{0,1:T(8,128)(2,1)}, u32[]{:S(2)}) copy-start(bf16[1024,448]{0,1:T(8,128)(2,1)} %param.7) | copy-start | bytes 2752516
  25.2 4.4 %copy-start.5 = (bf16[1,1024,64]{1,2,0:T(8,128)(2,1)S(1)}, bf16[1,1024,64]{1,2,0:T(8,128)(2,1)}, u32[]{:S(2)}) copy-start(bf16[1,1024,64]{1,2,0:T(8,128)(2,1)} %param.8) | copy-start | bytes 393220
  25.3 27.0 %all-to-all-start.1 = ((bf16[4,8,32,1024]{3,2,1,0:T(8,128)(2,1)}), bf16[4,8,32,1024]{3,2,1,0:T(8,128)(2,1)S(1)}, u32[]{:S(2)}, u32[]{:S(2)}) async-start(bf16[4,8,32,1024]{3,2,1,0:T(8,128)(2,1)} %broadcast_in_dim.30), calls=%async_computation.1 | async-start | bytes 4194304 | tf_op jit(solution)/shard_map/all_to_all | solution.py:22
  29.6 5.9 %copy-start.6 = (s32[2048,1]{0,1:T(1,128)S(1)}, s32[2048,1]{0,1:T(1,128)}, u32[]{:S(2)}) copy-start(s32[2048,1]{0,1:T(1,128)} %param.10) | copy-start | bytes 24580
  29.6 5.9 %copy-start.7 = (s32[64]{0:T(128)S(1)}, s32[64]{0:T(128)}, u32[]{:S(2)}) copy-start(s32[64]{0:T(128)} %param.11) | copy-start | bytes 772
  30.7 7.3 %collective-permute-start = (bf16[512,1024]{1,0:T(8,128)(2,1)}, bf16[512,1024]{1,0:T(8,128)(2,1)S(1)}, u32[]{:S(2)}, u32[]{:S(2)}) collective-permute-start(bf16[512,1024]{1,0:T(8,128)(2,1)} %pad_maximum_fusion), channel_id=1, source_target_pairs={{0,8},{8,0},{1,9},{9,1},{2,10},{10,2},{3,11},{11,3},{4,12},{12,4},... | collective-permute-start | bytes 3145736 | tf_op jit(solution)/shard_map/ppermute | solution.py:17
  38.0 14.5 %copy-start.2 = (bf16[512,1024]{1,0:T(8,128)(2,1)}, bf16[512,1024]{1,0:T(8,128)(2,1)S(1)}, u32[]{:S(2)}) copy-start(bf16[512,1024]{1,0:T(8,128)(2,1)S(1)} %collective-permute-done) | copy-start | bytes 3145732
  52.5 1.3 copy-start.1
  52.5 16.5 %copy-start.4 = (bf16[1024,448]{0,1:T(8,128)(2,1)S(1)}, bf16[1024,448]{0,1:T(8,128)(2,1)}, u32[]{:S(2)}) copy-start(bf16[1024,448]{0,1:T(8,128)(2,1)} %param.7) | copy-start | bytes 2752516
  53.8 15.1 %slice-start = ((bf16[512,1024]{1,0:T(8,128)(2,1)}), bf16[448,1024]{1,0:T(8,128)(2,1)S(1)}, s32[]{:S(2)}) async-start(bf16[512,1024]{1,0:T(8,128)(2,1)} %copy-done.2), calls=%async_computation.4 | async-start | bytes 1835008 | tf_op jit(solution)/shard_map/slice | solution.py:60
  55.9 23.9 %all-to-all-start.2 = ((f32[16,8,128]{2,1,0:T(8,128)}), f32[16,8,128]{2,1,0:T(8,128)S(1)}, u32[]{:S(2)}, u32[]{:S(2)}) async-start(f32[16,8,128]{2,1,0:T(8,128)} %reshape.133), calls=%async_computation.2 | async-start | bytes 131072 | tf_op jit(solution)/shard_map/all_to_all | solution.py:106
  72.6 1.8 %copy-start = (f32[896,8,128]{2,0,1:T(8,128)}, f32[896,8,128]{2,0,1:T(8,128)S(1)}, u32[]{:S(2)}) copy-start(f32[896,8,128]{2,0,1:T(8,128)S(1)} %fusion.1) | copy-start | bytes 11010052
  74.5 17.0 %collective-permute-start.1 = (bf16[896,128]{1,0:T(8,128)(2,1)S(1)}, bf16[896,128]{1,0:T(8,128)(2,1)S(1)}, u32[]{:S(2)}, u32[]{:S(2)}) collective-permute-start(bf16[896,128]{1,0:T(8,128)(2,1)S(1)} %get-tuple-element.9), channel_id=1, source_target_pairs={{0,1},{1,2},{2,3},{3,4},{4,5},{5,6},{6,7},{7,0},{8,9},{9,10},{10,1... | collective-permute-start | bytes 688136 | tf_op jit(solution)/shard_map/ppermute | solution.py:17
  77.6 18.1 %collective-permute-start.5 = (bf16[896,128]{1,0:T(8,128)(2,1)S(1)}, bf16[896,128]{1,0:T(8,128)(2,1)S(1)}, u32[]{:S(2)}, u32[]{:S(2)}) collective-permute-start(bf16[896,128]{1,0:T(8,128)(2,1)S(1)} %get-tuple-element.10), channel_id=1, source_target_pairs={{0,7},{1,0},{2,1},{3,2},{4,3},{5,4},{6,5},{7,6},{8,15},{9,8},{10,9... | collective-permute-start | bytes 688136 | tf_op jit(solution)/shard_map/ppermute | solution.py:17
  85.4 50.0 %all-to-all-start.3 = ((bf16[64,16,448]{2,1,0:T(8,128)(2,1)}), bf16[64,16,448]{2,1,0:T(8,128)(2,1)S(1)}, u32[]{:S(2)}, u32[]{:S(2)}) async-start(bf16[64,16,448]{2,1,0:T(8,128)(2,1)} %bitcast.57), calls=%async_computation.3 | async-start | bytes 2097152 | tf_op jit(solution)/shard_map/all_to_all | solution.py:111
  92.6 8.7 %collective-permute-start.2 = (bf16[896,128]{1,0:T(8,128)(2,1)S(1)}, bf16[896,128]{1,0:T(8,128)(2,1)S(1)}, u32[]{:S(2)}, u32[]{:S(2)}) collective-permute-start(bf16[896,128]{1,0:T(8,128)(2,1)S(1)} %fusion.15), channel_id=1, source_target_pairs={{0,1},{1,2},{2,3},{3,4},{4,5},{5,6},{6,7},{7,0},{8,9},{9,10},{10,1... | collective-permute-start | bytes 688136 | tf_op jit(solution)/shard_map/ppermute | solution.py:17
  102.5 8.9 %collective-permute-start.3 = (bf16[896,128]{1,0:T(8,128)(2,1)S(1)}, bf16[896,128]{1,0:T(8,128)(2,1)S(1)}, u32[]{:S(2)}, u32[]{:S(2)}) collective-permute-start(bf16[896,128]{1,0:T(8,128)(2,1)S(1)} %get-tuple-element.7), channel_id=1, source_target_pairs={{0,1},{1,2},{2,3},{3,4},{4,5},{5,6},{6,7},{7,0},{8,9},{9,10},{10,1... | collective-permute-start | bytes 688136 | tf_op jit(solution)/shard_map/ppermute | solution.py:17
  105.6 8.9 %collective-permute-start.6 = (bf16[896,128]{1,0:T(8,128)(2,1)S(1)}, bf16[896,128]{1,0:T(8,128)(2,1)S(1)}, u32[]{:S(2)}, u32[]{:S(2)}) collective-permute-start(bf16[896,128]{1,0:T(8,128)(2,1)S(1)} %get-tuple-element.8), channel_id=1, source_target_pairs={{0,7},{1,0},{2,1},{3,2},{4,3},{5,4},{6,5},{7,6},{8,15},{9,8},{10,9... | collective-permute-start | bytes 688136 | tf_op jit(solution)/shard_map/ppermute | solution.py:17
  115.8 8.3 %collective-permute-start.4 = (bf16[896,128]{1,0:T(8,128)(2,1)S(1)}, bf16[896,128]{1,0:T(8,128)(2,1)S(1)}, u32[]{:S(2)}, u32[]{:S(2)}) collective-permute-start(bf16[896,128]{1,0:T(8,128)(2,1)S(1)} %get-tuple-element.5), channel_id=1, source_target_pairs={{0,1},{1,2},{2,3},{3,4},{4,5},{5,6},{6,7},{7,0},{8,9},{9,10},{10,1... | collective-permute-start | bytes 688136 | tf_op jit(solution)/shard_map/ppermute | solution.py:17
  121.1 7.7 %collective-permute-start.7 = (bf16[896,128]{1,0:T(8,128)(2,1)S(1)}, bf16[896,128]{1,0:T(8,128)(2,1)S(1)}, u32[]{:S(2)}, u32[]{:S(2)}) collective-permute-start(bf16[896,128]{1,0:T(8,128)(2,1)S(1)} %get-tuple-element.6), channel_id=1, source_target_pairs={{0,7},{1,0},{2,1},{3,2},{4,3},{5,4},{6,5},{7,6},{8,15},{9,8},{10,9... | collective-permute-start | bytes 688136 | tf_op jit(solution)/shard_map/ppermute | solution.py:17
  130.0 6.5 %collective-permute-start.8 = (f32[448,128]{1,0:T(8,128)S(1)}, f32[448,128]{1,0:T(8,128)S(1)}, u32[]{:S(2)}, u32[]{:S(2)}) collective-permute-start(f32[448,128]{1,0:T(8,128)S(1)} %get-tuple-element.12), channel_id=1, source_target_pairs={{0,8},{8,0},{1,9},{9,1},{2,10},{10,2},{3,11},{11,3},{4,12},{12,4},... | collective-permute-start | bytes 688136 | tf_op jit(solution)/shard_map/ppermute | solution.py:17

commit v2 on v1

v2 whole, which is shorter than its diff:
```python
import functools

import jax
import jax.numpy as jnp
from jax import lax
from jax.sharding import Mesh
from jax.sharding import PartitionSpec as P

from jax.experimental import pallas as pl
from jax.experimental.pallas import tpu as pltpu


CAP = 16
ADAPTER_SCALE = 2.0
Y, X, C, ZH, ZL = "wide_y", "wide_x", "wide_c", "narrow_h", "narrow_l"
WIDE = (Y, X, C)
Z = (ZH, ZL)
BF16, F32 = jnp.bfloat16, jnp.float32
HIGHEST = lax.Precision.HIGHEST


def shifted(value, axis, step):
    size = lax.axis_size(axis)
    return lax.ppermute(value, axis, [(i, (i + step) % size) for i in range(size)])


def from_everyone(shard, axis):
    devices = lax.axis_size(axis)
    return lax.all_to_all(
        jnp.broadcast_to(shard[None], (devices, *shard.shape)), axis, 0, 0, tiled=True
    )


def sum_at_owner(parts):
    size = lax.axis_size(ZH)
    me = lax.axis_index(ZH)

    def own(offset):
        return lax.dynamic_index_in_dim(parts, (me + offset) % size, 0, keepdims=False)

    total = own(0)
    terms = [shifted(own(step).astype(BF16), ZH, step) for step in range(1, size)]
    for term in terms:
        total = total + term.astype(F32)
    return total


def expand_kernel(columns, terms_ref, factor_ref, out_ref, shrunk_ref):
    @pl.when(pl.program_id(0) == 0)
    def _():
        total = jnp.sum(terms_ref[...], axis=0)
        rank = total.shape[1] // 2
        half = total.shape[0]
        shrunk_ref[:half] = total[:, :rank]
        shrunk_ref[half:] = total[:, rank:]

    piece = jnp.dot(
        shrunk_ref[...].astype(BF16), factor_ref[...], preferred_element_type=F32
    )
    for i in range(out_ref.shape[0]):
        out_ref[i] = piece[:, i * columns : (i + 1) * columns].astype(BF16)


def expanded(terms, factor, pool, columns):
    together = 16
    rank, width = factor.shape
    return pl.pallas_call(
        functools.partial(expand_kernel, columns),
        grid=(pool // together,),
        in_specs=[
            pl.BlockSpec(terms.shape, lambda i: (0, 0, 0)),
            pl.BlockSpec((rank, together * columns), lambda i: (0, i)),
        ],
        out_specs=pl.BlockSpec((together, CAP, columns), lambda i: (i, 0, 0)),
        out_shape=jax.ShapeDtypeStruct((pool, CAP, columns), BF16),
        scratch_shapes=[pltpu.VMEM((CAP, rank), F32)],
        cost_estimate=pl.CostEstimate(
            flops=2 * CAP * rank * width, bytes_accessed=2 * (rank + CAP) * width, transcendentals=0
        ),
    )(terms, factor)


def per_device(activations, up_weight, shrink_pool, expand_pool, row_adapter, holder_slot):
    block_rows = activations.shape[0]
    columns = up_weight.shape[1]
    rank = shrink_pool.shape[2]
    pool = holder_slot.shape[0]
    n_z, n_x, n_c = lax.axis_size(Z), lax.axis_size(X), lax.axis_size(C)
    me_y, me_x, me_c, me_z = (lax.axis_index(a) for a in (Y, X, C, Z))
    me_zl = lax.axis_index(ZL)

    line_rows = from_everyone(activations, Y)

    own_shrink = shrink_pool[0].T
    near = jnp.concatenate(
        [own_shrink] + [shifted(own_shrink, X, step) for step in range(1, n_x)], axis=0
    )
    far = shifted(near, C, 1)

    own_weight = up_weight.T
    plane_weight = shifted(own_weight, ZL, 1)
    core_own = shifted(own_weight, C, 1)
    core_weights = core_own, shifted(plane_weight, C, 1)

    position = jnp.sum(
        jnp.where(
            row_adapter[:, 0][:, None] == jnp.arange(pool, dtype=jnp.int32)[None, :],
            holder_slot[None, :],
            0,
        ),
        axis=1,
    )
    grouped = position.reshape(n_z, -1)
    group_rows = grouped.shape[1]
    earlier = (
        jnp.arange(group_rows, dtype=jnp.int32)[:, None]
        > jnp.arange(group_rows, dtype=jnp.int32)[None, :]
    )
    place = jnp.sum(
        jnp.where(earlier[None] & (grouped[:, :, None] == grouped[:, None, :]), 1, 0), axis=2
    ).astype(jnp.int32)

    paired = line_rows.reshape(n_z // 2, 2, block_rows, -1)
    kept = lax.dynamic_index_in_dim(paired, me_zl, 1, keepdims=False)
    given = lax.dynamic_index_in_dim(paired, 1 - me_zl, 1, keepdims=False)
    taken = shifted(given, ZL, 1)
    blocks = jnp.stack([kept, taken])
    across = [blocks] + [shifted(blocks, X, step) for step in range(1, n_x)]

    def of_line(table):
        blocks = table.reshape(n_z, n_x * n_c, block_rows)
        return lax.dynamic_index_in_dim(blocks, me_x * n_c + me_c, 1, keepdims=False).reshape(-1)

    line_position, line_place = of_line(grouped), of_line(place)
    held_x = (me_x - jnp.arange(n_x, dtype=jnp.int32)) % n_x
    low = []
    for factors, core in ((near, me_c), (far, 1 - me_c)):
        held = (me_y * n_x + held_x) * n_c + core
        product = jnp.einsum("gik,nk->gin", line_rows, factors, preferred_element_type=F32)
        product = product.reshape(n_z * block_rows, n_x, rank)
        low.append(
            jnp.sum(
                jnp.where((line_position[:, None] == held[None])[..., None], product, 0.0), axis=1
            )
        )
    low = low[0] + low[1]
    line_group = jnp.arange(n_z * block_rows, dtype=jnp.int32) // block_rows
    local = line_position - me_y * (n_x * n_c)
    slots = n_x * n_c * n_z * CAP
    slot = jnp.where(
        (local >= 0) & (local < n_x * n_c), (local * n_z + line_group) * CAP + line_place, -1
    )
    half = CAP // 2
    slot_half = (slot // half) % 2
    slot_line = jnp.where(slot >= 0, (slot // CAP) * half + slot % half, -1)
    lines = jnp.arange(slots // 2, dtype=jnp.int32)[:, None]
    placed = jnp.concatenate(
        [
            ((lines == slot_line[None, :]) & (slot_half[None, :] == side)).astype(F32)
            for side in range(2)
        ],
        axis=1,
    )
    none = jnp.zeros_like(low)
    sides = jnp.concatenate(
        [jnp.concatenate([low, none], axis=1), jnp.concatenate([none, low], axis=1)], axis=0
    )
    packed = jnp.dot(placed, sides, precision=HIGHEST, preferred_element_type=F32)
    packed = packed.reshape(n_x * n_c * n_z, half, 2 * rank)
    gathered = lax.all_to_all(packed, (X, C, ZH, ZL), 0, 0, tiled=True)

    pieces = expanded(gathered, expand_pool[0], pool, columns)
    received = lax.all_to_all(pieces, WIDE, 0, 0, tiled=True)
    received = received.reshape(pool * CAP, columns)

    weights = [
        jnp.concatenate([own_weight, core_weights[0]], axis=0),
        jnp.concatenate([plane_weight, core_weights[1]], axis=0),
    ]
    rows = jnp.concatenate(across, axis=2)
    partial = sum(
        jnp.einsum("grk,nk->grn", rows[i], weights[i], preferred_element_type=F32)
        for i in range(2)
    )
    base = sum_at_owner(partial)
    mine = jnp.concatenate([base[:, :columns], shifted(base[:, columns:], C, 1)], axis=0)

    group_position = lax.dynamic_index_in_dim(grouped, me_z, 0, keepdims=False)
    group_place = lax.dynamic_index_in_dim(place, me_z, 0, keepdims=False)
    slot_of_row = group_position * CAP + group_place
    chosen = (
        jnp.arange(pool * CAP, dtype=jnp.int32)[:, None] == slot_of_row[None, :]
    ).astype(BF16)
    update = lax.dot_general(
        received, chosen, (((0,), (0,)), ((), ())), preferred_element_type=F32
    )
    row = jnp.arange(group_rows, dtype=jnp.int32)
    block = row // block_rows
    row_x, row_c = block // n_c, block % n_c
    source = (
        (row_c ^ me_c) * n_x + (me_x - row_x) % n_x
    ) * block_rows + row % block_rows
    spread = (jnp.arange(group_rows, dtype=jnp.int32)[:, None] == source[None, :]).astype(F32)
    base_rows = lax.dot_general(
        mine, spread, (((0,), (0,)), ((), ())), precision=HIGHEST, preferred_element_type=F32
    )
    return (base_rows + ADAPTER_SCALE * update).astype(BF16).T


def solution(mesh):
    finer = Mesh(mesh.devices.reshape(8, 4, 2, 4, 2), (Y, X, C, ZH, ZL))

    return jax.shard_map(
        per_device,
        mesh=finer,
        in_specs=(
            P(WIDE, Z),
            P(Z, WIDE),
            P(WIDE, Z, None),
            P(WIDE, None, None),
            P(),
            P(),
        ),
        out_specs=P(Z, WIDE),
        check_vma=False,
    )
```

time: 138 us -> 144 us (1.043)
  the two profiles are of different devices: /device:TPU:67 before, /device:TPU:65 now
where the time goes in v2:
time: 144 us; the launch traced here: 143 us
  starting transfers between devices  71.1 us (49%)
  waiting for transfers between devices  48 us (33%)
  matrix products  9.09 us (6%)
  other arithmetic  5.53 us (4%)
  Pallas kernels  4.67 us (3%)
  local copies, waits for them, and re-layouts  4.26 us (3%)
    ppermute x15, starting transfers between devices, shifted(): lax.ppermute(value, axis, [(i, (i + step) % size) for i in range(size)])  49.4 us
    ppermute x15, waiting for transfers between devices, shifted(): lax.ppermute(value, axis, [(i, (i + step) % size) for i in range(size)])  34.8 us
    all_to_all x1, waiting for transfers between devices, from_everyone(): lax.all_to_all(jnp.broadcast_to(shard[None], (devices, *shard.shape)), ax...  13.2 us
    all_to_all x1, starting transfers between devices, per_device(): gathered = lax.all_to_all(packed, (X, C, ZH, ZL), 0, 0, tiled=True)  12.7 us
    dot_general x2, matrix products, per_device(): jnp.einsum('grk,nk->grn', rows[i], weights[i], preferred_element_type=F32)  5.22 us
    pallas_call x1, Pallas kernels, expanded(): pl.pallas_call(functools.partial(expand_kernel, columns), grid=(pool // t...  4.67 us
    all_to_all x1, starting transfers between devices, per_device(): received = lax.all_to_all(pieces, WIDE, 0, 0, tiled=True)  4.55 us
    all_to_all x1, starting transfers between devices, from_everyone(): lax.all_to_all(jnp.broadcast_to(shard[None], (devices, *shard.shape)), ax...  4.52 us
  transfers between devices with their start and end apart: 18, of which 5 were waited for; matrix products, arithmetic and copies ran while one was open for 12% of the time, Pallas kernels for 3%

profile of v2, /device:TPU:65, one launch (start us, length us, event | category | flops | bytes accessed | tf_op | source)
XLA Modules:
  0.0 143.2 jit_solution(17379486193673577061)
XLA Ops:
  0.0 4.5 %collective-permute-start.13 = (bf16[64,1024]{1,0:T(8,128)(2,1)}, bf16[64,1024]{1,0:T(8,128)(2,1)S(1)}, u32[]{:S(2)}, u32[]{:S(2)}) collective-permute-start(bf16[64,1024]{1,0:T(8,128)(2,1)} %bitcast.64), channel_id=1, source_target_pairs={{0,48},{16,0},{32,16},{48,32},{1,49},{17,1},{33,17},{49,33},{2,50}... | collective-permute-start | bytes 393224 | tf_op jit(solution)/shard_map/ppermute | solution.py:24
  4.5 2.4 %collective-permute-start.12 = (bf16[64,1024]{1,0:T(8,128)(2,1)}, bf16[64,1024]{1,0:T(8,128)(2,1)S(1)}, u32[]{:S(2)}, u32[]{:S(2)}) collective-permute-start(bf16[64,1024]{1,0:T(8,128)(2,1)} %bitcast.65), channel_id=1, source_target_pairs={{0,32},{16,48},{32,0},{48,16},{1,33},{17,49},{33,1},{49,17},{2,34}... | collective-permute-start | bytes 393224 | tf_op jit(solution)/shard_map/ppermute | solution.py:24
  7.0 2.5 %collective-permute-start.11 = (bf16[64,1024]{1,0:T(8,128)(2,1)}, bf16[64,1024]{1,0:T(8,128)(2,1)S(1)}, u32[]{:S(2)}, u32[]{:S(2)}) collective-permute-start(bf16[64,1024]{1,0:T(8,128)(2,1)} %bitcast.66), channel_id=1, source_target_pairs={{0,16},{16,32},{32,48},{48,0},{1,17},{17,33},{33,49},{49,1},{2,18}... | collective-permute-start | bytes 393224 | tf_op jit(solution)/shard_map/ppermute | solution.py:24
  9.5 3.4 %collective-permute-start.4 = (bf16[448,1024]{1,0:T(8,128)(2,1)}, bf16[448,1024]{1,0:T(8,128)(2,1)}, u32[]{:S(2)}, u32[]{:S(2)}) collective-permute-start(bf16[448,1024]{1,0:T(8,128)(2,1)} %bitcast.71), channel_id=1, source_target_pairs={{0,8},{8,0},{1,9},{9,1},{2,10},{10,2},{3,11},{11,3},{4,12},{12,4},... | collective-permute-start | bytes 2752520 | tf_op jit(solution)/shard_map/ppermute | solution.py:24
  12.9 4.2 %collective-permute-start.5 = (bf16[448,1024]{1,0:T(8,128)(2,1)}, bf16[448,1024]{1,0:T(8,128)(2,1)}, u32[]{:S(2)}, u32[]{:S(2)}) collective-permute-start(bf16[448,1024]{1,0:T(8,128)(2,1)} %bitcast.72), channel_id=1, source_target_pairs={{0,1},{1,0},{2,3},{3,2},{4,5},{5,4},{6,7},{7,6},{8,9},{9,8},{10,11... | collective-permute-start | bytes 2752520 | tf_op jit(solution)/shard_map/ppermute | solution.py:24
  17.1 1.7 %broadcast_in_dim.43 = bf16[8,32,1024]{2,1,0:T(8,128)(2,1)} broadcast(bf16[32,1024]{1,0:T(8,128)(2,1)} %param.6), dimensions={1,2} | broadcast | bytes 589824 | tf_op jit(solution)/shard_map/broadcast_in_dim | solution.py:30
  18.8 4.5 %all-to-all-start = ((bf16[8,32,1024]{2,1,0:T(8,128)(2,1)}), bf16[8,32,1024]{2,1,0:T(8,128)(2,1)S(1)}, u32[]{:S(2)}, u32[]{:S(2)}) async-start(bf16[8,32,1024]{2,1,0:T(8,128)(2,1)} %broadcast_in_dim.43), calls=%async_computation | async-start | bytes 1048576 | tf_op jit(solution)/shard_map/all_to_all | solution.py:29
  23.4 0.9 select_reduce_fusion.3
  24.4 0.9 select_reduce_fusion
  25.9 2.2 %collective-permute-start.14 = (bf16[256,1024]{1,0:T(8,128)(2,1)S(1)}, bf16[256,1024]{1,0:T(8,128)(2,1)S(1)}, u32[]{:S(2)}, u32[]{:S(2)}) collective-permute-start(bf16[256,1024]{1,0:T(8,128)(2,1)S(1)} %pad_maximum_fusion.2), channel_id=1, source_target_pairs={{0,8},{8,0},{1,9},{9,1},{2,10},{10,2},{3,11},{11,3},{4,12},{12,4},... | collective-permute-start | bytes 1572872 | tf_op jit(solution)/shard_map/ppermute | solution.py:24
  28.2 13.2 %all-to-all-done = bf16[8,32,1024]{2,1,0:T(8,128)(2,1)S(1)} async-done(((bf16[8,32,1024]{2,1,0:T(8,128)(2,1)}), bf16[8,32,1024]{2,1,0:T(8,128)(2,1)S(1)}, u32[]{:S(2)}, u32[]{:S(2)}) %all-to-all-start) | async-done | bytes 524320 | tf_op jit(solution)/shard_map/all_to_all | solution.py:29
  42.0 3.3 %collective-permute-start = (bf16[4,32,1024]{2,1,0:T(8,128)(2,1)S(1)}, bf16[4,32,1024]{2,1,0:T(8,128)(2,1)S(1)}, u32[]{:S(2)}, u32[]{:S(2)}) collective-permute-start(bf16[4,32,1024]{2,1,0:T(8,128)(2,1)S(1)} %get-tuple-element.12), channel_id=1, source_target_pairs={{0,1},{1,0},{2,3},{3,2},{4,5},{5,4},{6,7},{7,6},{8,9},{9,8},{10,11... | collective-permute-start | bytes 786440 | tf_op jit(solution)/shard_map/ppermute | solution.py:24
  46.9 1.3 convolution_bitcast_fusion
  48.3 12.7 %all-to-all-start.1 = ((f32[64,8,128]{2,1,0:T(8,128)}), f32[64,8,128]{2,1,0:T(8,128)S(1)}, u32[]{:S(2)}, u32[]{:S(2)}) async-start(f32[64,8,128]{2,1,0:T(8,128)} %convolution_bitcast_fusion), calls=%async_computation.1 | async-start | bytes 524288 | tf_op jit(solution)/shard_map/all_to_all | solution.py:170
  61.0 4.6 %collective-permute-start.3 = (bf16[2,4,32,1024]{3,2,1,0:T(8,128)(2,1)S(1)}, bf16[2,4,32,1024]{3,2,1,0:T(8,128)(2,1)S(1)}, u32[]{:S(2)}, u32[]{:S(2)}) collective-permute-start(bf16[2,4,32,1024]{3,2,1,0:T(8,128)(2,1)S(1)} %pad_maximum_fusion.1), channel_id=1, source_target_pairs={{0,48},{16,0},{32,16},{48,32},{1,49},{17,1},{33,17},{49,33},{2,50}... | collective-permute-start | bytes 1572872 | tf_op jit(solution)/shard_map/ppermute | solution.py:24
  65.6 2.3 %collective-permute-start.2 = (bf16[2,4,32,1024]{3,2,1,0:T(8,128)(2,1)S(1)}, bf16[2,4,32,1024]{3,2,1,0:T(8,128)(2,1)S(1)}, u32[]{:S(2)}, u32[]{:S(2)}) collective-permute-start(bf16[2,4,32,1024]{3,2,1,0:T(8,128)(2,1)S(1)} %pad_maximum_fusion.1), channel_id=1, source_target_pairs={{0,32},{16,48},{32,0},{48,16},{1,33},{17,49},{33,1},{49,17},{2,34}... | collective-permute-start | bytes 1572872 | tf_op jit(solution)/shard_map/ppermute | solution.py:24
  67.9 2.6 %collective-permute-start.1 = (bf16[2,4,32,1024]{3,2,1,0:T(8,128)(2,1)S(1)}, bf16[2,4,32,1024]{3,2,1,0:T(8,128)(2,1)}, u32[]{:S(2)}, u32[]{:S(2)}) collective-permute-start(bf16[2,4,32,1024]{3,2,1,0:T(8,128)(2,1)S(1)} %pad_maximum_fusion.1), channel_id=1, source_target_pairs={{0,16},{16,32},{32,48},{48,0},{1,17},{17,33},{33,49},{49,1},{2,18}... | collective-permute-start | bytes 1572872 | tf_op jit(solution)/shard_map/ppermute | solution.py:24
  70.5 3.1 %collective-permute-start.6 = (bf16[448,1024]{1,0:T(8,128)(2,1)}, bf16[448,1024]{1,0:T(8,128)(2,1)}, u32[]{:S(2)}, u32[]{:S(2)}) collective-permute-start(bf16[448,1024]{1,0:T(8,128)(2,1)} %collective-permute-done.5), channel_id=1, source_target_pairs={{0,8},{8,0},{1,9},{9,1},{2,10},{10,2},{3,11},{11,3},{4,12},{12,4},... | collective-permute-start | bytes 2752520 | tf_op jit(solution)/shard_map/ppermute | solution.py:24
  74.3 4.7 %shard_map.64 = bf16[64,16,448]{2,1,0:T(8,128)(2,1)} custom-call(f32[64,8,128]{2,1,0:T(8,128)} %copy-done, bf16[64,28672]{1,0:T(8,128)(2,1)} %bitcast.60), custom_call_target="tpu_custom_call" | custom-call | flops 58720256 | bytes 4587520 | tf_op jit(solution)/shard_map/pallas_call | solution.py:67
  79.0 4.5 %all-to-all-start.2 = ((bf16[64,16,448]{2,1,0:T(8,128)(2,1)}), bf16[64,16,448]{2,1,0:T(8,128)(2,1)S(1)}, u32[]{:S(2)}, u32[]{:S(2)}) async-start(bf16[64,16,448]{2,1,0:T(8,128)(2,1)} %shard_map.64), calls=%async_computation.2 | async-start | bytes 2097152 | tf_op jit(solution)/shard_map/all_to_all | solution.py:173
  83.6 15.6 %collective-permute-done.1 = bf16[2,4,32,1024]{3,2,1,0:T(8,128)(2,1)} collective-permute-done((bf16[2,4,32,1024]{3,2,1,0:T(8,128)(2,1)S(1)}, bf16[2,4,32,1024]{3,2,1,0:T(8,128)(2,1)}, u32[]{:S(2)}, u32[]{:S(2)}) %collective-permute-start.1) | collective-permute-done | bytes 524320 | tf_op jit(solution)/shard_map/ppermute | solution.py:24
  99.3 1.1 pad_maximum_fusion
  100.5 2.5 %fusion = f32[4,128,896]{2,1,0:T(8,128)S(1)} fusion(bf16[448,1024]{1,0:T(8,128)(2,1)} %collective-permute-done.4, bf16[448,1024]{1,0:T(8,128)(2,1)S(1)} %bitcast.73, bf16[2,4,128,1024]{3,2,1,0:T(8,128)(2,1)S(1)} %pad_maximum_fusion), kind=kOutput, calls=%fused_computation.3 | convolution fusion | flops 943194112 | bytes 4718592 | tf_op jit(solution)/shard_map/grk,nk->grn/dot_general | solution.py:182
  102.9 2.8 %fusion.6 = f32[4,128,896]{2,1,0:T(8,128)S(1)} fusion(f32[4,128,896]{2,1,0:T(8,128)S(1)} %fusion, bf16[448,1024]{1,0:T(8,128)(2,1)} %collective-permute-done.6, bf16[448,1024]{1,0:T(8,128)(2,1)} %collective-permute-done.5, bf16[2,4,128,1024]{3,2,1,0:T(8,128)(2,1)S(1)} %pad_maximum_fusion), kind=kOutput, calls=%fused_computation.10 | convolution fusion | flops 943652864 | bytes 6553600 | tf_op jit(solution)/shard_map/grk,nk->grn/dot_general | solution.py:182
  106.6 4.2 %collective-permute-start.9 = (bf16[128,896]{1,0:T(8,128)(2,1)}, bf16[128,896]{1,0:T(8,128)(2,1)S(1)}, u32[]{:S(2)}, u32[]{:S(2)}) collective-permute-start(bf16[128,896]{1,0:T(8,128)(2,1)} %get-tuple-element.9), channel_id=1, source_target_pairs={{0,6},{2,0},{4,2},{6,4},{1,7},{3,1},{5,3},{7,5},{8,14},{10,8},{12,... | collective-permute-start | bytes 688136 | tf_op jit(solution)/shard_map/ppermute | solution.py:24
  110.8 5.0 %collective-permute-start.8 = (bf16[128,896]{1,0:T(8,128)(2,1)}, bf16[128,896]{1,0:T(8,128)(2,1)}, u32[]{:S(2)}, u32[]{:S(2)}) collective-permute-start(bf16[128,896]{1,0:T(8,128)(2,1)} %get-tuple-element.10), channel_id=1, source_target_pairs={{0,4},{2,6},{4,0},{6,2},{1,5},{3,7},{5,1},{7,3},{8,12},{10,14},{12... | collective-permute-start | bytes 688136 | tf_op jit(solution)/shard_map/ppermute | solution.py:24
  115.7 2.7 %collective-permute-start.7 = (bf16[128,896]{1,0:T(8,128)(2,1)S(1)}, bf16[128,896]{1,0:T(8,128)(2,1)}, u32[]{:S(2)}, u32[]{:S(2)}) collective-permute-start(bf16[128,896]{1,0:T(8,128)(2,1)S(1)} %get-tuple-element.8), channel_id=1, source_target_pairs={{0,2},{2,4},{4,6},{6,0},{1,3},{3,5},{5,7},{7,1},{8,10},{10,12},{12... | collective-permute-start | bytes 688136 | tf_op jit(solution)/shard_map/ppermute | solution.py:24
  118.5 15.9 %collective-permute-done.8 = bf16[128,896]{1,0:T(8,128)(2,1)} collective-permute-done((bf16[128,896]{1,0:T(8,128)(2,1)}, bf16[128,896]{1,0:T(8,128)(2,1)}, u32[]{:S(2)}, u32[]{:S(2)}) %collective-permute-start.8) | collective-permute-done | bytes 229408 | tf_op jit(solution)/shard_map/ppermute | solution.py:24
  134.4 2.7 %collective-permute-done.7 = bf16[128,896]{1,0:T(8,128)(2,1)} collective-permute-done((bf16[128,896]{1,0:T(8,128)(2,1)S(1)}, bf16[128,896]{1,0:T(8,128)(2,1)}, u32[]{:S(2)}, u32[]{:S(2)}) %collective-permute-start.7) | collective-permute-done | bytes 229408 | tf_op jit(solution)/shard_map/ppermute | solution.py:24
  137.1 1.1 fusion.20
  138.4 2.4 %collective-permute-start.10 = (f32[128,448]{1,0:T(8,128)S(1)}, f32[128,448]{1,0:T(8,128)S(1)}, u32[]{:S(2)}, u32[]{:S(2)}) collective-permute-start(f32[128,448]{1,0:T(8,128)S(1)} %get-tuple-element.14), channel_id=1, source_target_pairs={{0,8},{8,0},{1,9},{9,1},{2,10},{10,2},{3,11},{11,3},{4,12},{12,4},... | collective-permute-start | bytes 688136 | tf_op jit(solution)/shard_map/ppermute | solution.py:24
  141.9 1.3 fusion.7
  (48 shorter events, 5.9 us)
Async XLA Ops:
  0.0 25.8 %copy-start.1 = (bf16[1,1024,64]{1,2,0:T(8,128)(2,1)S(1)}, bf16[1,1024,64]{1,2,0:T(8,128)(2,1)}, u32[]{:S(2)}) copy-start(bf16[1,1024,64]{1,2,0:T(8,128)(2,1)} %param.8) | copy-start | bytes 393220
  0.0 25.8 %collective-permute-start.13 = (bf16[64,1024]{1,0:T(8,128)(2,1)}, bf16[64,1024]{1,0:T(8,128)(2,1)S(1)}, u32[]{:S(2)}, u32[]{:S(2)}) collective-permute-start(bf16[64,1024]{1,0:T(8,128)(2,1)} %bitcast.64), channel_id=1, source_target_pairs={{0,48},{16,0},{32,16},{48,32},{1,49},{17,1},{33,17},{49,33},{2,50}... | collective-permute-start | bytes 393224 | tf_op jit(solution)/shard_map/ppermute | solution.py:24
  4.5 21.3 %collective-permute-start.12 = (bf16[64,1024]{1,0:T(8,128)(2,1)}, bf16[64,1024]{1,0:T(8,128)(2,1)S(1)}, u32[]{:S(2)}, u32[]{:S(2)}) collective-permute-start(bf16[64,1024]{1,0:T(8,128)(2,1)} %bitcast.65), channel_id=1, source_target_pairs={{0,32},{16,48},{32,0},{48,16},{1,33},{17,49},{33,1},{49,17},{2,34}... | collective-permute-start | bytes 393224 | tf_op jit(solution)/shard_map/ppermute | solution.py:24
  7.0 18.9 %collective-permute-start.11 = (bf16[64,1024]{1,0:T(8,128)(2,1)}, bf16[64,1024]{1,0:T(8,128)(2,1)S(1)}, u32[]{:S(2)}, u32[]{:S(2)}) collective-permute-start(bf16[64,1024]{1,0:T(8,128)(2,1)} %bitcast.66), channel_id=1, source_target_pairs={{0,16},{16,32},{32,48},{48,0},{1,17},{17,33},{33,49},{49,1},{2,18}... | collective-permute-start | bytes 393224 | tf_op jit(solution)/shard_map/ppermute | solution.py:24
  9.5 91.0 %collective-permute-start.4 = (bf16[448,1024]{1,0:T(8,128)(2,1)}, bf16[448,1024]{1,0:T(8,128)(2,1)}, u32[]{:S(2)}, u32[]{:S(2)}) collective-permute-start(bf16[448,1024]{1,0:T(8,128)(2,1)} %bitcast.71), channel_id=1, source_target_pairs={{0,8},{8,0},{1,9},{9,1},{2,10},{10,2},{3,11},{11,3},{4,12},{12,4},... | collective-permute-start | bytes 2752520 | tf_op jit(solution)/shard_map/ppermute | solution.py:24
  12.9 57.6 %collective-permute-start.5 = (bf16[448,1024]{1,0:T(8,128)(2,1)}, bf16[448,1024]{1,0:T(8,128)(2,1)}, u32[]{:S(2)}, u32[]{:S(2)}) collective-permute-start(bf16[448,1024]{1,0:T(8,128)(2,1)} %bitcast.72), channel_id=1, source_target_pairs={{0,1},{1,0},{2,3},{3,2},{4,5},{5,4},{6,7},{7,6},{8,9},{9,8},{10,11... | collective-permute-start | bytes 2752520 | tf_op jit(solution)/shard_map/ppermute | solution.py:24
  18.8 22.6 %all-to-all-start = ((bf16[8,32,1024]{2,1,0:T(8,128)(2,1)}), bf16[8,32,1024]{2,1,0:T(8,128)(2,1)S(1)}, u32[]{:S(2)}, u32[]{:S(2)}) async-start(bf16[8,32,1024]{2,1,0:T(8,128)(2,1)} %broadcast_in_dim.43), calls=%async_computation | async-start | bytes 1048576 | tf_op jit(solution)/shard_map/all_to_all | solution.py:29
  25.9 19.4 %collective-permute-start.14 = (bf16[256,1024]{1,0:T(8,128)(2,1)S(1)}, bf16[256,1024]{1,0:T(8,128)(2,1)S(1)}, u32[]{:S(2)}, u32[]{:S(2)}) collective-permute-start(bf16[256,1024]{1,0:T(8,128)(2,1)S(1)} %pad_maximum_fusion.2), channel_id=1, source_target_pairs={{0,8},{8,0},{1,9},{9,1},{2,10},{10,2},{3,11},{11,3},{4,12},{12,4},... | collective-permute-start | bytes 1572872 | tf_op jit(solution)/shard_map/ppermute | solution.py:24
  42.0 19.0 %collective-permute-start = (bf16[4,32,1024]{2,1,0:T(8,128)(2,1)S(1)}, bf16[4,32,1024]{2,1,0:T(8,128)(2,1)S(1)}, u32[]{:S(2)}, u32[]{:S(2)}) collective-permute-start(bf16[4,32,1024]{2,1,0:T(8,128)(2,1)S(1)} %get-tuple-element.12), channel_id=1, source_target_pairs={{0,1},{1,0},{2,3},{3,2},{4,5},{5,4},{6,7},{7,6},{8,9},{9,8},{10,11... | collective-permute-start | bytes 786440 | tf_op jit(solution)/shard_map/ppermute | solution.py:24
  48.3 25.3 %all-to-all-start.1 = ((f32[64,8,128]{2,1,0:T(8,128)}), f32[64,8,128]{2,1,0:T(8,128)S(1)}, u32[]{:S(2)}, u32[]{:S(2)}) async-start(f32[64,8,128]{2,1,0:T(8,128)} %convolution_bitcast_fusion), calls=%async_computation.1 | async-start | bytes 524288 | tf_op jit(solution)/shard_map/all_to_all | solution.py:170
  61.0 22.6 %collective-permute-start.3 = (bf16[2,4,32,1024]{3,2,1,0:T(8,128)(2,1)S(1)}, bf16[2,4,32,1024]{3,2,1,0:T(8,128)(2,1)S(1)}, u32[]{:S(2)}, u32[]{:S(2)}) collective-permute-start(bf16[2,4,32,1024]{3,2,1,0:T(8,128)(2,1)S(1)} %pad_maximum_fusion.1), channel_id=1, source_target_pairs={{0,48},{16,0},{32,16},{48,32},{1,49},{17,1},{33,17},{49,33},{2,50}... | collective-permute-start | bytes 1572872 | tf_op jit(solution)/shard_map/ppermute | solution.py:24
  65.6 18.0 %collective-permute-start.2 = (bf16[2,4,32,1024]{3,2,1,0:T(8,128)(2,1)S(1)}, bf16[2,4,32,1024]{3,2,1,0:T(8,128)(2,1)S(1)}, u32[]{:S(2)}, u32[]{:S(2)}) collective-permute-start(bf16[2,4,32,1024]{3,2,1,0:T(8,128)(2,1)S(1)} %pad_maximum_fusion.1), channel_id=1, source_target_pairs={{0,32},{16,48},{32,0},{48,16},{1,33},{17,49},{33,1},{49,17},{2,34}... | collective-permute-start | bytes 1572872 | tf_op jit(solution)/shard_map/ppermute | solution.py:24
  67.9 31.4 %collective-permute-start.1 = (bf16[2,4,32,1024]{3,2,1,0:T(8,128)(2,1)S(1)}, bf16[2,4,32,1024]{3,2,1,0:T(8,128)(2,1)}, u32[]{:S(2)}, u32[]{:S(2)}) collective-permute-start(bf16[2,4,32,1024]{3,2,1,0:T(8,128)(2,1)S(1)} %pad_maximum_fusion.1), channel_id=1, source_target_pairs={{0,16},{16,32},{32,48},{48,0},{1,17},{17,33},{33,49},{49,1},{2,18}... | collective-permute-start | bytes 1572872 | tf_op jit(solution)/shard_map/ppermute | solution.py:24
  70.5 32.4 %collective-permute-start.6 = (bf16[448,1024]{1,0:T(8,128)(2,1)}, bf16[448,1024]{1,0:T(8,128)(2,1)}, u32[]{:S(2)}, u32[]{:S(2)}) collective-permute-start(bf16[448,1024]{1,0:T(8,128)(2,1)} %collective-permute-done.5), channel_id=1, source_target_pairs={{0,8},{8,0},{1,9},{9,1},{2,10},{10,2},{3,11},{11,3},{4,12},{12,4},... | collective-permute-start | bytes 2752520 | tf_op jit(solution)/shard_map/ppermute | solution.py:24
  73.6 0.7 copy-start
  79.0 61.8 %all-to-all-start.2 = ((bf16[64,16,448]{2,1,0:T(8,128)(2,1)}), bf16[64,16,448]{2,1,0:T(8,128)(2,1)S(1)}, u32[]{:S(2)}, u32[]{:S(2)}) async-start(bf16[64,16,448]{2,1,0:T(8,128)(2,1)} %shard_map.64), calls=%async_computation.2 | async-start | bytes 2097152 | tf_op jit(solution)/shard_map/all_to_all | solution.py:173
  83.6 16.8 %copy-start.2 = (bf16[1024,448]{0,1:T(8,128)(2,1)S(1)}, bf16[1024,448]{0,1:T(8,128)(2,1)}, u32[]{:S(2)}) copy-start(bf16[1024,448]{0,1:T(8,128)(2,1)} %param.7) | copy-start | bytes 2752516
  106.6 11.9 %collective-permute-start.9 = (bf16[128,896]{1,0:T(8,128)(2,1)}, bf16[128,896]{1,0:T(8,128)(2,1)S(1)}, u32[]{:S(2)}, u32[]{:S(2)}) collective-permute-start(bf16[128,896]{1,0:T(8,128)(2,1)} %get-tuple-element.9), channel_id=1, source_target_pairs={{0,6},{2,0},{4,2},{6,4},{1,7},{3,1},{5,3},{7,5},{8,14},{10,8},{12,... | collective-permute-start | bytes 688136 | tf_op jit(solution)/shard_map/ppermute | solution.py:24
  110.8 23.6 %collective-permute-start.8 = (bf16[128,896]{1,0:T(8,128)(2,1)}, bf16[128,896]{1,0:T(8,128)(2,1)}, u32[]{:S(2)}, u32[]{:S(2)}) collective-permute-start(bf16[128,896]{1,0:T(8,128)(2,1)} %get-tuple-element.10), channel_id=1, source_target_pairs={{0,4},{2,6},{4,0},{6,2},{1,5},{3,7},{5,1},{7,3},{8,12},{10,14},{12... | collective-permute-start | bytes 688136 | tf_op jit(solution)/shard_map/ppermute | solution.py:24
  115.7 21.4 %collective-permute-start.7 = (bf16[128,896]{1,0:T(8,128)(2,1)S(1)}, bf16[128,896]{1,0:T(8,128)(2,1)}, u32[]{:S(2)}, u32[]{:S(2)}) collective-permute-start(bf16[128,896]{1,0:T(8,128)(2,1)S(1)} %get-tuple-element.8), channel_id=1, source_target_pairs={{0,2},{2,4},{4,6},{6,0},{1,3},{3,5},{5,7},{7,1},{8,10},{10,12},{12... | collective-permute-start | bytes 688136 | tf_op jit(solution)/shard_map/ppermute | solution.py:24
  138.4 3.5 %collective-permute-start.10 = (f32[128,448]{1,0:T(8,128)S(1)}, f32[128,448]{1,0:T(8,128)S(1)}, u32[]{:S(2)}, u32[]{:S(2)}) collective-permute-start(f32[128,448]{1,0:T(8,128)S(1)} %get-tuple-element.14), channel_id=1, source_target_pairs={{0,8},{8,0},{1,9},{9,1},{2,10},{10,2},{3,11},{11,3},{4,12},{12,4},... | collective-permute-start | bytes 688136 | tf_op jit(solution)/shard_map/ppermute | solution.py:24

commit v3 on v2

--- a/solution.py
+++ b/solution.py
@@ -45,38 +45,32 @@
     return total
 
 
-def expand_kernel(columns, terms_ref, factor_ref, out_ref, shrunk_ref):
-    @pl.when(pl.program_id(0) == 0)
-    def _():
-        total = jnp.sum(terms_ref[...], axis=0)
-        rank = total.shape[1] // 2
-        half = total.shape[0]
-        shrunk_ref[:half] = total[:, :rank]
-        shrunk_ref[half:] = total[:, rank:]
-
-    piece = jnp.dot(
-        shrunk_ref[...].astype(BF16), factor_ref[...], preferred_element_type=F32
-    )
-    for i in range(out_ref.shape[0]):
-        out_ref[i] = piece[:, i * columns : (i + 1) * columns].astype(BF16)
+def expand_kernel(columns, terms_ref, factor_ref, out_ref):
+    total = jnp.sum(terms_ref[...], axis=0)
+    rank = total.shape[1] // 2
+    shrunk = jnp.concatenate([total[:, :rank], total[:, rank:]], axis=0).astype(BF16)
+    together = 8
+    for first in range(0, out_ref.shape[0], together):
+        piece = jnp.dot(
+            shrunk,
+            factor_ref[:, first * columns : (first + together) * columns],
+            preferred_element_type=F32,
+        )
+        for i in range(together):
+            out_ref[first + i] = piece[:, i * columns : (i + 1) * columns].astype(BF16)
 
 
 def expanded(terms, factor, pool, columns):
-    together = 16
     rank, width = factor.shape
     return pl.pallas_call(
         functools.partial(expand_kernel, columns),
-        grid=(pool // together,),
-        in_specs=[
-            pl.BlockSpec(terms.shape, lambda i: (0, 0, 0)),
-            pl.BlockSpec((rank, together * columns), lambda i: (0, i)),
-        ],
-        out_specs=pl.BlockSpec((together, CAP, columns), lambda i: (i, 0, 0)),
+        in_specs=[pl.BlockSpec(memory_space=pltpu.VMEM)] * 2,
+        out_specs=pl.BlockSpec(memory_space=pltpu.VMEM),
         out_shape=jax.ShapeDtypeStruct((pool, CAP, columns), BF16),
-        scratch_shapes=[pltpu.VMEM((CAP, rank), F32)],
         cost_estimate=pl.CostEstimate(
             flops=2 * CAP * rank * width, bytes_accessed=2 * (rank + CAP) * width, transcendentals=0
         ),
+        compiler_params=pltpu.CompilerParams(vmem_limit_bytes=24 << 20),
     )(terms, factor)
 
 

time: 144 us -> 145 us (level)
  Pallas kernels: 4.67 us -> 1.78 us
  waiting for transfers between devices: 48 us -> 50.5 us
    pallas_call x1, Pallas kernels: 4.67 us -> 1.78 us  [expanded(): pl.pallas_call(functools.partial(expand_kernel, columns), in_specs=[pl.Bl...]
    ppermute x15, waiting for transfers between devices: 34.8 us -> 37.3 us  [shifted(): lax.ppermute(value, axis, [(i, (i + step) % size) for i in range(size)])]
  transfers between devices with their start and end apart: 18 -> 18, of which waited for: 5 -> 6; matrix products, arithmetic and copies ran while one was open for 12% -> 12% of each run, Pallas kernels for 3% -> 1%
where the time goes in v3:
time: 145 us; the launch traced here: 144 us
  starting transfers between devices  71.1 us (49%)
  waiting for transfers between devices  50.5 us (35%)
  matrix products  9.09 us (6%)
  local copies, waits for them, and re-layouts  5.58 us (4%)
  other arithmetic  5.53 us (4%)
  Pallas kernels  1.78 us (1%)
    ppermute x15, starting transfers between devices, shifted(): lax.ppermute(value, axis, [(i, (i + step) % size) for i in range(size)])  49.3 us
    ppermute x15, waiting for transfers between devices, shifted(): lax.ppermute(value, axis, [(i, (i + step) % size) for i in range(size)])  37.3 us
    all_to_all x1, waiting for transfers between devices, from_everyone(): lax.all_to_all(jnp.broadcast_to(shard[None], (devices, *shard.shape)), ax...  13.2 us
    all_to_all x1, starting transfers between devices, per_device(): gathered = lax.all_to_all(packed, (X, C, ZH, ZL), 0, 0, tiled=True)  12.7 us
    dot_general x2, matrix products, per_device(): jnp.einsum('grk,nk->grn', rows[i], weights[i], preferred_element_type=F32)  5.22 us
    all_to_all x1, starting transfers between devices, per_device(): received = lax.all_to_all(pieces, WIDE, 0, 0, tiled=True)  4.55 us
    all_to_all x1, starting transfers between devices, from_everyone(): lax.all_to_all(jnp.broadcast_to(shard[None], (devices, *shard.shape)), ax...  4.52 us
  transfers between devices with their start and end apart: 18, of which 6 were waited for; matrix products, arithmetic and copies ran while one was open for 12% of the time, Pallas kernels for 1%

profile of v3, /device:TPU:65, one launch (start us, length us, event | category | flops | bytes accessed | tf_op | source)
XLA Modules:
  0.0 144.1 jit_solution(13266134560441004311)
XLA Ops:
  0.0 4.5 %collective-permute-start.13 = (bf16[64,1024]{1,0:T(8,128)(2,1)}, bf16[64,1024]{1,0:T(8,128)(2,1)S(1)}, u32[]{:S(2)}, u32[]{:S(2)}) collective-permute-start(bf16[64,1024]{1,0:T(8,128)(2,1)} %bitcast.64), channel_id=1, source_target_pairs={{0,48},{16,0},{32,16},{48,32},{1,49},{17,1},{33,17},{49,33},{2,50}... | collective-permute-start | bytes 393224 | tf_op jit(solution)/shard_map/ppermute | solution.py:24
  4.5 2.4 %collective-permute-start.12 = (bf16[64,1024]{1,0:T(8,128)(2,1)}, bf16[64,1024]{1,0:T(8,128)(2,1)S(1)}, u32[]{:S(2)}, u32[]{:S(2)}) collective-permute-start(bf16[64,1024]{1,0:T(8,128)(2,1)} %bitcast.65), channel_id=1, source_target_pairs={{0,32},{16,48},{32,0},{48,16},{1,33},{17,49},{33,1},{49,17},{2,34}... | collective-permute-start | bytes 393224 | tf_op jit(solution)/shard_map/ppermute | solution.py:24
  7.0 2.5 %collective-permute-start.11 = (bf16[64,1024]{1,0:T(8,128)(2,1)}, bf16[64,1024]{1,0:T(8,128)(2,1)S(1)}, u32[]{:S(2)}, u32[]{:S(2)}) collective-permute-start(bf16[64,1024]{1,0:T(8,128)(2,1)} %bitcast.66), channel_id=1, source_target_pairs={{0,16},{16,32},{32,48},{48,0},{1,17},{17,33},{33,49},{49,1},{2,18}... | collective-permute-start | bytes 393224 | tf_op jit(solution)/shard_map/ppermute | solution.py:24
  9.5 3.4 %collective-permute-start.4 = (bf16[448,1024]{1,0:T(8,128)(2,1)}, bf16[448,1024]{1,0:T(8,128)(2,1)}, u32[]{:S(2)}, u32[]{:S(2)}) collective-permute-start(bf16[448,1024]{1,0:T(8,128)(2,1)} %bitcast.71), channel_id=1, source_target_pairs={{0,8},{8,0},{1,9},{9,1},{2,10},{10,2},{3,11},{11,3},{4,12},{12,4},... | collective-permute-start | bytes 2752520 | tf_op jit(solution)/shard_map/ppermute | solution.py:24
  12.9 4.2 %collective-permute-start.5 = (bf16[448,1024]{1,0:T(8,128)(2,1)}, bf16[448,1024]{1,0:T(8,128)(2,1)}, u32[]{:S(2)}, u32[]{:S(2)}) collective-permute-start(bf16[448,1024]{1,0:T(8,128)(2,1)} %bitcast.72), channel_id=1, source_target_pairs={{0,1},{1,0},{2,3},{3,2},{4,5},{5,4},{6,7},{7,6},{8,9},{9,8},{10,11... | collective-permute-start | bytes 2752520 | tf_op jit(solution)/shard_map/ppermute | solution.py:24
  17.1 1.7 %broadcast_in_dim.43 = bf16[8,32,1024]{2,1,0:T(8,128)(2,1)} broadcast(bf16[32,1024]{1,0:T(8,128)(2,1)} %param.6), dimensions={1,2} | broadcast | bytes 589824 | tf_op jit(solution)/shard_map/broadcast_in_dim | solution.py:30
  18.8 4.5 %all-to-all-start = ((bf16[8,32,1024]{2,1,0:T(8,128)(2,1)}), bf16[8,32,1024]{2,1,0:T(8,128)(2,1)S(1)}, u32[]{:S(2)}, u32[]{:S(2)}) async-start(bf16[8,32,1024]{2,1,0:T(8,128)(2,1)} %broadcast_in_dim.43), calls=%async_computation | async-start | bytes 1048576 | tf_op jit(solution)/shard_map/all_to_all | solution.py:29
  24.4 0.9 select_reduce_fusion
  25.9 2.2 %collective-permute-start.14 = (bf16[256,1024]{1,0:T(8,128)(2,1)S(1)}, bf16[256,1024]{1,0:T(8,128)(2,1)S(1)}, u32[]{:S(2)}, u32[]{:S(2)}) collective-permute-start(bf16[256,1024]{1,0:T(8,128)(2,1)S(1)} %pad_maximum_fusion.2), channel_id=1, source_target_pairs={{0,8},{8,0},{1,9},{9,1},{2,10},{10,2},{3,11},{11,3},{4,12},{12,4},... | collective-permute-start | bytes 1572872 | tf_op jit(solution)/shard_map/ppermute | solution.py:24
  28.2 13.2 %all-to-all-done = bf16[8,32,1024]{2,1,0:T(8,128)(2,1)S(1)} async-done(((bf16[8,32,1024]{2,1,0:T(8,128)(2,1)}), bf16[8,32,1024]{2,1,0:T(8,128)(2,1)S(1)}, u32[]{:S(2)}, u32[]{:S(2)}) %all-to-all-start) | async-done | bytes 524320 | tf_op jit(solution)/shard_map/all_to_all | solution.py:29
  42.0 3.3 %collective-permute-start = (bf16[4,32,1024]{2,1,0:T(8,128)(2,1)S(1)}, bf16[4,32,1024]{2,1,0:T(8,128)(2,1)S(1)}, u32[]{:S(2)}, u32[]{:S(2)}) collective-permute-start(bf16[4,32,1024]{2,1,0:T(8,128)(2,1)S(1)} %get-tuple-element.12), channel_id=1, source_target_pairs={{0,1},{1,0},{2,3},{3,2},{4,5},{5,4},{6,7},{7,6},{8,9},{9,8},{10,11... | collective-permute-start | bytes 786440 | tf_op jit(solution)/shard_map/ppermute | solution.py:24
  46.9 1.3 convolution_bitcast_fusion
  48.3 12.7 %all-to-all-start.1 = ((f32[64,8,128]{2,1,0:T(8,128)}), f32[64,8,128]{2,1,0:T(8,128)S(1)}, u32[]{:S(2)}, u32[]{:S(2)}) async-start(f32[64,8,128]{2,1,0:T(8,128)} %convolution_bitcast_fusion), calls=%async_computation.1 | async-start | bytes 524288 | tf_op jit(solution)/shard_map/all_to_all | solution.py:164
  61.0 4.6 %collective-permute-start.3 = (bf16[2,4,32,1024]{3,2,1,0:T(8,128)(2,1)S(1)}, bf16[2,4,32,1024]{3,2,1,0:T(8,128)(2,1)S(1)}, u32[]{:S(2)}, u32[]{:S(2)}) collective-permute-start(bf16[2,4,32,1024]{3,2,1,0:T(8,128)(2,1)S(1)} %pad_maximum_fusion.1), channel_id=1, source_target_pairs={{0,48},{16,0},{32,16},{48,32},{1,49},{17,1},{33,17},{49,33},{2,50}... | collective-permute-start | bytes 1572872 | tf_op jit(solution)/shard_map/ppermute | solution.py:24
  65.6 2.3 %collective-permute-start.2 = (bf16[2,4,32,1024]{3,2,1,0:T(8,128)(2,1)S(1)}, bf16[2,4,32,1024]{3,2,1,0:T(8,128)(2,1)S(1)}, u32[]{:S(2)}, u32[]{:S(2)}) collective-permute-start(bf16[2,4,32,1024]{3,2,1,0:T(8,128)(2,1)S(1)} %pad_maximum_fusion.1), channel_id=1, source_target_pairs={{0,32},{16,48},{32,0},{48,16},{1,33},{17,49},{33,1},{49,17},{2,34}... | collective-permute-start | bytes 1572872 | tf_op jit(solution)/shard_map/ppermute | solution.py:24
  67.9 2.6 %collective-permute-start.1 = (bf16[2,4,32,1024]{3,2,1,0:T(8,128)(2,1)S(1)}, bf16[2,4,32,1024]{3,2,1,0:T(8,128)(2,1)}, u32[]{:S(2)}, u32[]{:S(2)}) collective-permute-start(bf16[2,4,32,1024]{3,2,1,0:T(8,128)(2,1)S(1)} %pad_maximum_fusion.1), channel_id=1, source_target_pairs={{0,16},{16,32},{32,48},{48,0},{1,17},{17,33},{33,49},{49,1},{2,18}... | collective-permute-start | bytes 1572872 | tf_op jit(solution)/shard_map/ppermute | solution.py:24
  70.5 3.1 %collective-permute-start.6 = (bf16[448,1024]{1,0:T(8,128)(2,1)}, bf16[448,1024]{1,0:T(8,128)(2,1)}, u32[]{:S(2)}, u32[]{:S(2)}) collective-permute-start(bf16[448,1024]{1,0:T(8,128)(2,1)} %collective-permute-done.5), channel_id=1, source_target_pairs={{0,8},{8,0},{1,9},{9,1},{2,10},{10,2},{3,11},{11,3},{4,12},{12,4},... | collective-permute-start | bytes 2752520 | tf_op jit(solution)/shard_map/ppermute | solution.py:24
  73.6 2.0 %copy-done = bf16[1,64,28672]{2,1,0:T(8,128)(2,1)S(1)} copy-done((bf16[1,64,28672]{2,1,0:T(8,128)(2,1)S(1)}, bf16[1,64,28672]{2,1,0:T(8,128)(2,1)}, u32[]{:S(2)}) %copy-start) | copy-done | bytes 3670040
  75.7 1.8 %shard_map.64 = bf16[64,16,448]{2,1,0:T(8,128)(2,1)} custom-call(f32[64,8,128]{2,1,0:T(8,128)S(1)} %all-to-all-done.1.terms_ref, bf16[64,28672]{1,0:T(8,128)(2,1)S(1)} %bitcast.59), custom_call_target="tpu_custom_call" | custom-call | flops 58720256 | bytes 4587520 | tf_op jit(solution)/shard_map/pallas_call | solution.py:65
  77.4 4.5 %all-to-all-start.2 = ((bf16[64,16,448]{2,1,0:T(8,128)(2,1)}), bf16[64,16,448]{2,1,0:T(8,128)(2,1)S(1)}, u32[]{:S(2)}, u32[]{:S(2)}) async-start(bf16[64,16,448]{2,1,0:T(8,128)(2,1)} %shard_map.64), calls=%async_computation.2 | async-start | bytes 2097152 | tf_op jit(solution)/shard_map/all_to_all | solution.py:167
  82.6 17.6 %collective-permute-done.1 = bf16[2,4,32,1024]{3,2,1,0:T(8,128)(2,1)} collective-permute-done((bf16[2,4,32,1024]{3,2,1,0:T(8,128)(2,1)S(1)}, bf16[2,4,32,1024]{3,2,1,0:T(8,128)(2,1)}, u32[]{:S(2)}, u32[]{:S(2)}) %collective-permute-start.1) | collective-permute-done | bytes 524320 | tf_op jit(solution)/shard_map/ppermute | solution.py:24
  100.2 1.1 pad_maximum_fusion
  101.4 2.5 %fusion = f32[4,128,896]{2,1,0:T(8,128)S(1)} fusion(bf16[448,1024]{1,0:T(8,128)(2,1)} %collective-permute-done.4, bf16[448,1024]{1,0:T(8,128)(2,1)S(1)} %bitcast.73, bf16[2,4,128,1024]{3,2,1,0:T(8,128)(2,1)S(1)} %pad_maximum_fusion), kind=kOutput, calls=%fused_computation.3 | convolution fusion | flops 943194112 | bytes 4718592 | tf_op jit(solution)/shard_map/grk,nk->grn/dot_general | solution.py:176
  103.8 2.8 %fusion.6 = f32[4,128,896]{2,1,0:T(8,128)S(1)} fusion(f32[4,128,896]{2,1,0:T(8,128)S(1)} %fusion, bf16[448,1024]{1,0:T(8,128)(2,1)} %collective-permute-done.6, bf16[448,1024]{1,0:T(8,128)(2,1)} %collective-permute-done.5, bf16[2,4,128,1024]{3,2,1,0:T(8,128)(2,1)S(1)} %pad_maximum_fusion), kind=kOutput, calls=%fused_computation.10 | convolution fusion | flops 943652864 | bytes 6553600 | tf_op jit(solution)/shard_map/grk,nk->grn/dot_general | solution.py:176
  107.5 4.1 %collective-permute-start.9 = (bf16[128,896]{1,0:T(8,128)(2,1)}, bf16[128,896]{1,0:T(8,128)(2,1)S(1)}, u32[]{:S(2)}, u32[]{:S(2)}) collective-permute-start(bf16[128,896]{1,0:T(8,128)(2,1)} %get-tuple-element.9), channel_id=1, source_target_pairs={{0,6},{2,0},{4,2},{6,4},{1,7},{3,1},{5,3},{7,5},{8,14},{10,8},{12,... | collective-permute-start | bytes 688136 | tf_op jit(solution)/shard_map/ppermute | solution.py:24
  111.6 5.0 %collective-permute-start.8 = (bf16[128,896]{1,0:T(8,128)(2,1)}, bf16[128,896]{1,0:T(8,128)(2,1)}, u32[]{:S(2)}, u32[]{:S(2)}) collective-permute-start(bf16[128,896]{1,0:T(8,128)(2,1)} %get-tuple-element.10), channel_id=1, source_target_pairs={{0,4},{2,6},{4,0},{6,2},{1,5},{3,7},{5,1},{7,3},{8,12},{10,14},{12... | collective-permute-start | bytes 688136 | tf_op jit(solution)/shard_map/ppermute | solution.py:24
  116.6 2.7 %collective-permute-start.7 = (bf16[128,896]{1,0:T(8,128)(2,1)S(1)}, bf16[128,896]{1,0:T(8,128)(2,1)}, u32[]{:S(2)}, u32[]{:S(2)}) collective-permute-start(bf16[128,896]{1,0:T(8,128)(2,1)S(1)} %get-tuple-element.8), channel_id=1, source_target_pairs={{0,2},{2,4},{4,6},{6,0},{1,3},{3,5},{5,7},{7,1},{8,10},{10,12},{12... | collective-permute-start | bytes 688136 | tf_op jit(solution)/shard_map/ppermute | solution.py:24
  119.4 15.9 %collective-permute-done.8 = bf16[128,896]{1,0:T(8,128)(2,1)} collective-permute-done((bf16[128,896]{1,0:T(8,128)(2,1)}, bf16[128,896]{1,0:T(8,128)(2,1)}, u32[]{:S(2)}, u32[]{:S(2)}) %collective-permute-start.8) | collective-permute-done | bytes 229408 | tf_op jit(solution)/shard_map/ppermute | solution.py:24
  135.3 2.7 %collective-permute-done.7 = bf16[128,896]{1,0:T(8,128)(2,1)} collective-permute-done((bf16[128,896]{1,0:T(8,128)(2,1)S(1)}, bf16[128,896]{1,0:T(8,128)(2,1)}, u32[]{:S(2)}, u32[]{:S(2)}) %collective-permute-start.7) | collective-permute-done | bytes 229408 | tf_op jit(solution)/shard_map/ppermute | solution.py:24
  138.0 1.1 fusion.20
  139.3 2.4 %collective-permute-start.10 = (f32[128,448]{1,0:T(8,128)S(1)}, f32[128,448]{1,0:T(8,128)S(1)}, u32[]{:S(2)}, u32[]{:S(2)}) collective-permute-start(f32[128,448]{1,0:T(8,128)S(1)} %get-tuple-element.14), channel_id=1, source_target_pairs={{0,8},{8,0},{1,9},{9,1},{2,10},{10,2},{3,11},{11,3},{4,12},{12,4},... | collective-permute-start | bytes 688136 | tf_op jit(solution)/shard_map/ppermute | solution.py:24
  142.8 1.3 fusion.7
  (48 shorter events, 6.5 us)
Async XLA Ops:
  0.0 25.8 %copy-start.1 = (bf16[1,1024,64]{1,2,0:T(8,128)(2,1)S(1)}, bf16[1,1024,64]{1,2,0:T(8,128)(2,1)}, u32[]{:S(2)}) copy-start(bf16[1,1024,64]{1,2,0:T(8,128)(2,1)} %param.8) | copy-start | bytes 393220
  0.0 25.8 %collective-permute-start.13 = (bf16[64,1024]{1,0:T(8,128)(2,1)}, bf16[64,1024]{1,0:T(8,128)(2,1)S(1)}, u32[]{:S(2)}, u32[]{:S(2)}) collective-permute-start(bf16[64,1024]{1,0:T(8,128)(2,1)} %bitcast.64), channel_id=1, source_target_pairs={{0,48},{16,0},{32,16},{48,32},{1,49},{17,1},{33,17},{49,33},{2,50}... | collective-permute-start | bytes 393224 | tf_op jit(solution)/shard_map/ppermute | solution.py:24
  4.5 21.3 %collective-permute-start.12 = (bf16[64,1024]{1,0:T(8,128)(2,1)}, bf16[64,1024]{1,0:T(8,128)(2,1)S(1)}, u32[]{:S(2)}, u32[]{:S(2)}) collective-permute-start(bf16[64,1024]{1,0:T(8,128)(2,1)} %bitcast.65), channel_id=1, source_target_pairs={{0,32},{16,48},{32,0},{48,16},{1,33},{17,49},{33,1},{49,17},{2,34}... | collective-permute-start | bytes 393224 | tf_op jit(solution)/shard_map/ppermute | solution.py:24
  7.0 18.9 %collective-permute-start.11 = (bf16[64,1024]{1,0:T(8,128)(2,1)}, bf16[64,1024]{1,0:T(8,128)(2,1)S(1)}, u32[]{:S(2)}, u32[]{:S(2)}) collective-permute-start(bf16[64,1024]{1,0:T(8,128)(2,1)} %bitcast.66), channel_id=1, source_target_pairs={{0,16},{16,32},{32,48},{48,0},{1,17},{17,33},{33,49},{49,1},{2,18}... | collective-permute-start | bytes 393224 | tf_op jit(solution)/shard_map/ppermute | solution.py:24
  9.5 91.9 %collective-permute-start.4 = (bf16[448,1024]{1,0:T(8,128)(2,1)}, bf16[448,1024]{1,0:T(8,128)(2,1)}, u32[]{:S(2)}, u32[]{:S(2)}) collective-permute-start(bf16[448,1024]{1,0:T(8,128)(2,1)} %bitcast.71), channel_id=1, source_target_pairs={{0,8},{8,0},{1,9},{9,1},{2,10},{10,2},{3,11},{11,3},{4,12},{12,4},... | collective-permute-start | bytes 2752520 | tf_op jit(solution)/shard_map/ppermute | solution.py:24
  12.9 57.6 %collective-permute-start.5 = (bf16[448,1024]{1,0:T(8,128)(2,1)}, bf16[448,1024]{1,0:T(8,128)(2,1)}, u32[]{:S(2)}, u32[]{:S(2)}) collective-permute-start(bf16[448,1024]{1,0:T(8,128)(2,1)} %bitcast.72), channel_id=1, source_target_pairs={{0,1},{1,0},{2,3},{3,2},{4,5},{5,4},{6,7},{7,6},{8,9},{9,8},{10,11... | collective-permute-start | bytes 2752520 | tf_op jit(solution)/shard_map/ppermute | solution.py:24
  18.8 22.6 %all-to-all-start = ((bf16[8,32,1024]{2,1,0:T(8,128)(2,1)}), bf16[8,32,1024]{2,1,0:T(8,128)(2,1)S(1)}, u32[]{:S(2)}, u32[]{:S(2)}) async-start(bf16[8,32,1024]{2,1,0:T(8,128)(2,1)} %broadcast_in_dim.43), calls=%async_computation | async-start | bytes 1048576 | tf_op jit(solution)/shard_map/all_to_all | solution.py:29
  25.9 19.4 %collective-permute-start.14 = (bf16[256,1024]{1,0:T(8,128)(2,1)S(1)}, bf16[256,1024]{1,0:T(8,128)(2,1)S(1)}, u32[]{:S(2)}, u32[]{:S(2)}) collective-permute-start(bf16[256,1024]{1,0:T(8,128)(2,1)S(1)} %pad_maximum_fusion.2), channel_id=1, source_target_pairs={{0,8},{8,0},{1,9},{9,1},{2,10},{10,2},{3,11},{11,3},{4,12},{12,4},... | collective-permute-start | bytes 1572872 | tf_op jit(solution)/shard_map/ppermute | solution.py:24
  42.0 19.0 %collective-permute-start = (bf16[4,32,1024]{2,1,0:T(8,128)(2,1)S(1)}, bf16[4,32,1024]{2,1,0:T(8,128)(2,1)S(1)}, u32[]{:S(2)}, u32[]{:S(2)}) collective-permute-start(bf16[4,32,1024]{2,1,0:T(8,128)(2,1)S(1)} %get-tuple-element.12), channel_id=1, source_target_pairs={{0,1},{1,0},{2,3},{3,2},{4,5},{5,4},{6,7},{7,6},{8,9},{9,8},{10,11... | collective-permute-start | bytes 786440 | tf_op jit(solution)/shard_map/ppermute | solution.py:24
  48.3 25.3 %all-to-all-start.1 = ((f32[64,8,128]{2,1,0:T(8,128)}), f32[64,8,128]{2,1,0:T(8,128)S(1)}, u32[]{:S(2)}, u32[]{:S(2)}) async-start(f32[64,8,128]{2,1,0:T(8,128)} %convolution_bitcast_fusion), calls=%async_computation.1 | async-start | bytes 524288 | tf_op jit(solution)/shard_map/all_to_all | solution.py:164
  61.0 21.0 %collective-permute-start.3 = (bf16[2,4,32,1024]{3,2,1,0:T(8,128)(2,1)S(1)}, bf16[2,4,32,1024]{3,2,1,0:T(8,128)(2,1)S(1)}, u32[]{:S(2)}, u32[]{:S(2)}) collective-permute-start(bf16[2,4,32,1024]{3,2,1,0:T(8,128)(2,1)S(1)} %pad_maximum_fusion.1), channel_id=1, source_target_pairs={{0,48},{16,0},{32,16},{48,32},{1,49},{17,1},{33,17},{49,33},{2,50}... | collective-permute-start | bytes 1572872 | tf_op jit(solution)/shard_map/ppermute | solution.py:24
  65.6 16.9 %collective-permute-start.2 = (bf16[2,4,32,1024]{3,2,1,0:T(8,128)(2,1)S(1)}, bf16[2,4,32,1024]{3,2,1,0:T(8,128)(2,1)S(1)}, u32[]{:S(2)}, u32[]{:S(2)}) collective-permute-start(bf16[2,4,32,1024]{3,2,1,0:T(8,128)(2,1)S(1)} %pad_maximum_fusion.1), channel_id=1, source_target_pairs={{0,32},{16,48},{32,0},{48,16},{1,33},{17,49},{33,1},{49,17},{2,34}... | collective-permute-start | bytes 1572872 | tf_op jit(solution)/shard_map/ppermute | solution.py:24
  67.9 32.3 %collective-permute-start.1 = (bf16[2,4,32,1024]{3,2,1,0:T(8,128)(2,1)S(1)}, bf16[2,4,32,1024]{3,2,1,0:T(8,128)(2,1)}, u32[]{:S(2)}, u32[]{:S(2)}) collective-permute-start(bf16[2,4,32,1024]{3,2,1,0:T(8,128)(2,1)S(1)} %pad_maximum_fusion.1), channel_id=1, source_target_pairs={{0,16},{16,32},{32,48},{48,0},{1,17},{17,33},{33,49},{49,1},{2,18}... | collective-permute-start | bytes 1572872 | tf_op jit(solution)/shard_map/ppermute | solution.py:24
  70.5 33.3 %collective-permute-start.6 = (bf16[448,1024]{1,0:T(8,128)(2,1)}, bf16[448,1024]{1,0:T(8,128)(2,1)}, u32[]{:S(2)}, u32[]{:S(2)}) collective-permute-start(bf16[448,1024]{1,0:T(8,128)(2,1)} %collective-permute-done.5), channel_id=1, source_target_pairs={{0,8},{8,0},{1,9},{9,1},{2,10},{10,2},{3,11},{11,3},{4,12},{12,4},... | collective-permute-start | bytes 2752520 | tf_op jit(solution)/shard_map/ppermute | solution.py:24
  73.6 2.0 %copy-start = (bf16[1,64,28672]{2,1,0:T(8,128)(2,1)S(1)}, bf16[1,64,28672]{2,1,0:T(8,128)(2,1)}, u32[]{:S(2)}) copy-start(bf16[1,64,28672]{2,1,0:T(8,128)(2,1)} %param.9) | copy-start | bytes 11010052
  77.4 64.2 %all-to-all-start.2 = ((bf16[64,16,448]{2,1,0:T(8,128)(2,1)}), bf16[64,16,448]{2,1,0:T(8,128)(2,1)S(1)}, u32[]{:S(2)}, u32[]{:S(2)}) async-start(bf16[64,16,448]{2,1,0:T(8,128)(2,1)} %shard_map.64), calls=%async_computation.2 | async-start | bytes 2097152 | tf_op jit(solution)/shard_map/all_to_all | solution.py:167
  82.0 19.3 %copy-start.2 = (bf16[1024,448]{0,1:T(8,128)(2,1)S(1)}, bf16[1024,448]{0,1:T(8,128)(2,1)}, u32[]{:S(2)}) copy-start(bf16[1024,448]{0,1:T(8,128)(2,1)} %param.7) | copy-start | bytes 2752516
  107.5 11.9 %collective-permute-start.9 = (bf16[128,896]{1,0:T(8,128)(2,1)}, bf16[128,896]{1,0:T(8,128)(2,1)S(1)}, u32[]{:S(2)}, u32[]{:S(2)}) collective-permute-start(bf16[128,896]{1,0:T(8,128)(2,1)} %get-tuple-element.9), channel_id=1, source_target_pairs={{0,6},{2,0},{4,2},{6,4},{1,7},{3,1},{5,3},{7,5},{8,14},{10,8},{12,... | collective-permute-start | bytes 688136 | tf_op jit(solution)/shard_map/ppermute | solution.py:24
  111.6 23.7 %collective-permute-start.8 = (bf16[128,896]{1,0:T(8,128)(2,1)}, bf16[128,896]{1,0:T(8,128)(2,1)}, u32[]{:S(2)}, u32[]{:S(2)}) collective-permute-start(bf16[128,896]{1,0:T(8,128)(2,1)} %get-tuple-element.10), channel_id=1, source_target_pairs={{0,4},{2,6},{4,0},{6,2},{1,5},{3,7},{5,1},{7,3},{8,12},{10,14},{12... | collective-permute-start | bytes 688136 | tf_op jit(solution)/shard_map/ppermute | solution.py:24
  116.6 21.4 %collective-permute-start.7 = (bf16[128,896]{1,0:T(8,128)(2,1)S(1)}, bf16[128,896]{1,0:T(8,128)(2,1)}, u32[]{:S(2)}, u32[]{:S(2)}) collective-permute-start(bf16[128,896]{1,0:T(8,128)(2,1)S(1)} %get-tuple-element.8), channel_id=1, source_target_pairs={{0,2},{2,4},{4,6},{6,0},{1,3},{3,5},{5,7},{7,1},{8,10},{10,12},{12... | collective-permute-start | bytes 688136 | tf_op jit(solution)/shard_map/ppermute | solution.py:24
  139.3 3.5 %collective-permute-start.10 = (f32[128,448]{1,0:T(8,128)S(1)}, f32[128,448]{1,0:T(8,128)S(1)}, u32[]{:S(2)}, u32[]{:S(2)}) collective-permute-start(f32[128,448]{1,0:T(8,128)S(1)} %get-tuple-element.14), channel_id=1, source_target_pairs={{0,8},{8,0},{1,9},{9,1},{2,10},{10,2},{3,11},{11,3},{4,12},{12,4},... | collective-permute-start | bytes 688136 | tf_op jit(solution)/shard_map/ppermute | solution.py:24
